TPU v7x, 256 devices: a whole 4x4x8 slice. The times are simulated.
256 devices in a mesh: kz: 16 (over y_hi, x, core), ky: 16 (over z, y_lo).
Axes of the slice: x: 4, y: 4 (y_hi: 2, y_lo: 2; y = y_hi * 2 + y_lo), z: 8, core: 2. Of those that a mesh axis runs over, the one named last changes fastest.
Arguments:
- slice_re: bfloat16 [256, 512, 512], P('kz', 'ky'), may hold values from -6 to 6
- slice_im: bfloat16 [256, 512, 512], P('kz', 'ky'), may hold values from -6 to 6
- slice_ctf: bfloat16 [256, 512, 512], P('kz', 'ky'), may hold values from -1 to 1
- slice_dest: int32 [256, 1], P('kz'), may hold values from 0 to 15; in each aligned block of 16 rows (0 to 15, 16 to 31, ...) at most 4 rows name the same one
- slice_plane: int32 [256], P('kz'), may hold values from 0 to 3
- helix_index: int32 [256], P('kz'), may hold values from 0 to 7
- slice_tilt: bfloat16 [256], P('kz'), may hold values from -2 to 2
- slice_shift: bfloat16 [2, 256], P(None, 'kz'), may hold values from 0 to 1
Outputs:
- folded: float32 [3, 64, 1024, 1024], P(None, 'kz', 'ky')
Inputs may be any that keep to these rules, and one draw needn't show every extreme that they name: `slice_dest`: within each aligned block of 16 slices (the slices of one kz slab), at most 4 name the same slab, a bound that some block reaches of them.
All inputs are finite; a program needn't handle non-finite values.
Results may differ from a plain program's by a relative error of at most 0.0049.
Values may be sent and summed in bfloat16 or wider, within the bound.
A program may use at most 128 MiB of HBM per device.

v0:
```python
import jax
import jax.numpy as jnp
from jax import lax
from jax.sharding import PartitionSpec as P

ZD = 4
MZ = 4
MY = 1
GROUP = 8
CAP = 4
ZE = 12


kernel_beta = 7.4
kernel_reach = 2.0
twist_step = 0.37


def passed_along(shard, axis, by):
    size = lax.axis_size(axis)
    pairs = [(i, i + by) for i in range(size) if 0 <= i + by < size]
    return lax.ppermute(shard, axis, pairs)


def shifted(block, axis, distance):
    devices = range(lax.axis_size(axis))
    route = [((i - distance) % len(devices), i) for i in devices]
    return lax.ppermute(block, axis, route)


def from_partner(shard, axis, distance):
    return lax.ppermute(shard, axis, [(i, i ^ 1 << distance) for i in range(lax.axis_size(axis))])


def bessel_zero(value):
    quarter = value * value * 0.25
    term = jnp.ones_like(value)
    total = term
    for order in range(1, 26):
        term = term * quarter / float(order * order)
        total = total + term
    return total


def kaiser(distance):
    inside = jnp.clip(1.0 - (distance / kernel_reach) ** 2, 0.0, 1.0)
    scale = bessel_zero(jnp.asarray(kernel_beta, distance.dtype)) - 1.0
    return (bessel_zero(kernel_beta * jnp.sqrt(inside)) - 1.0) / scale


def spread_x(portion, offset_x):
    slice_width = portion.shape[-1]
    grid_width = 2 * slice_width
    columns = jnp.arange(slice_width)[:, None]
    cells = jnp.arange(grid_width)[None, :]
    lag = ((cells - 2 * columns + grid_width // 2) % grid_width - grid_width // 2).astype(
        jnp.float32
    )
    table = kaiser(lag[None] - offset_x[:, None, None]).astype(jnp.bfloat16)
    return jnp.einsum("gcuv,gvx->gcux", portion, table, preferred_element_type=jnp.float32).astype(
        jnp.bfloat16
    )


def per_device(
    slice_re, slice_im, slice_ctf, slice_dest, slice_plane, helix_index, slice_tilt, slice_shift
):
    slab_count = lax.axis_size("kz")
    block_count = lax.axis_size("ky")
    slab_index = lax.axis_index("kz")
    row_index = lax.axis_index("ky")
    held_count = slice_re.shape[0]
    strip_rows = slice_re.shape[1]
    slice_width = slice_re.shape[2]
    grid_width = 2 * slice_width
    block_rows = 2 * strip_rows
    extent_rows = block_rows + 2 * MY
    slot_count = slab_count * CAP
    ctf = slice_ctf.astype(jnp.float32)
    data = jnp.stack(
        [ctf * slice_re.astype(jnp.float32), ctf * slice_im.astype(jnp.float32), ctf * ctf], axis=1
    ).astype(jnp.bfloat16)
    ones = jnp.ones((held_count,), jnp.float32)
    zeros = jnp.zeros((held_count,), jnp.float32)
    geometry = jnp.stack(
        [
            slice_plane.astype(jnp.float32),
            helix_index.astype(jnp.float32),
            ones,
            slice_tilt.astype(jnp.float32),
            slice_shift[0].astype(jnp.float32),
            slice_shift[1].astype(jnp.float32),
            zeros,
            zeros,
        ],
        axis=1,
    ).astype(jnp.bfloat16)
    target = slice_dest[:, 0]
    onehot = (target[:, None] == jnp.arange(slab_count)[None, :]).astype(jnp.int32)
    ranking = jnp.sum((jnp.cumsum(onehot, axis=0) - 1) * onehot, axis=1)
    position = target * CAP + ranking
    matches = (jnp.arange(slot_count)[:, None] == position[None, :]).astype(jnp.int32)
    occupied = jnp.sum(matches, axis=1) > 0
    source_row = jnp.sum(matches * jnp.arange(held_count)[None, :], axis=1)

    def to_slots(values):
        picked = jnp.take(values, source_row, axis=0)
        keep = occupied.reshape((slot_count,) + (1,) * (values.ndim - 1))
        return jnp.where(keep, picked, jnp.zeros_like(picked))

    payload, arrived = (
        lax.all_to_all(to_slots(data), "kz", split_axis=0, concat_axis=0, tiled=True),
        lax.all_to_all(to_slots(geometry), "kz", split_axis=0, concat_axis=0, tiled=True),
    )
    live_flags = arrived[:, 2].astype(jnp.int32)
    order = jnp.argsort(1 - live_flags, stable=True)
    payload = jnp.take(payload, order, axis=0)
    arrived = jnp.take(arrived, order, axis=0)
    block_total = (jnp.sum(live_flags) + GROUP - 1) // GROUP
    rows_local = jnp.arange(strip_rows)
    rows_global = row_index * strip_rows + rows_local
    levels = (jnp.arange(ZE) - MZ).astype(jnp.float32)
    lines = jnp.arange(extent_rows)
    lag_rows = (lines[:, None] - MY - 2 * rows_local[None, :]).astype(jnp.float32)
    band_planes = slab_index * ZD + jnp.arange(ZE) - MZ

    def spread_block(block_index, volume):
        first = block_index * GROUP
        portion = lax.dynamic_slice_in_dim(payload, first, GROUP, 0)
        shape_info = lax.dynamic_slice_in_dim(arrived, first, GROUP, 0).astype(jnp.float32)
        portion = spread_x(portion, shape_info[:, 5])
        plane = shape_info[:, 0]
        helix_int = shape_info[:, 1].astype(jnp.int32)
        tilt = shape_info[:, 3]
        offset_y = shape_info[:, 4]
        centre = plane[:, None] + tilt[:, None] * (rows_global - slice_width // 2).astype(
            jnp.float32
        )[None, :] / (slice_width // 2)
        along_z = kaiser(levels[None, :, None] - centre[:, None, :])
        along_y = kaiser(lag_rows[None] - offset_y[:, None, None])
        joint = along_z[:, :, None, :] * along_y[:, None, :, :]
        angle = twist_step * (helix_int[:, None] * band_planes[None, :]).astype(jnp.float32)
        kreal = (joint * jnp.cos(angle)[:, :, None, None]).astype(jnp.bfloat16)
        kimag = (joint * jnp.sin(angle)[:, :, None, None]).astype(jnp.bfloat16)
        kweight = joint.astype(jnp.bfloat16)
        left_side = jnp.stack(
            [jnp.stack([kreal, -kimag], axis=1), jnp.stack([kimag, kreal], axis=1)], axis=0
        )
        complex_part = jnp.einsum(
            "ogczyu,gcux->ozyx", left_side, portion[:, 0:2], preferred_element_type=jnp.float32
        )
        weight_part = jnp.einsum(
            "gzyu,gux->zyx", kweight, portion[:, 2], preferred_element_type=jnp.float32
        )
        return volume + jnp.concatenate([complex_part, weight_part[None]], axis=0)

    volume = jnp.zeros((3, ZE, extent_rows, grid_width), jnp.float32)
    volume = lax.fori_loop(0, block_total, spread_block, volume)
    middle = volume[:, MZ : MZ + ZD]
    middle = middle + passed_along(volume[:, MZ + ZD :], "kz", 1)
    middle = middle + passed_along(volume[:, :MZ], "kz", -1)
    centre_rows = middle[:, :, MY : MY + block_rows]
    from_below = shifted(middle[:, :, MY + block_rows :].astype(jnp.bfloat16), "ky", 1).astype(
        jnp.float32
    )
    from_above = shifted(middle[:, :, :MY].astype(jnp.bfloat16), "ky", -1).astype(jnp.float32)
    centre_rows = centre_rows.at[:, :, :MY].add(from_below)
    centre_rows = centre_rows.at[:, :, block_rows - MY :].add(from_above)
    half = centre_rows.astype(jnp.bfloat16)
    mirror = half[:, ::-1, ::-1, ::-1]
    for bit_number in range(slab_count.bit_length() - 1):
        mirror = from_partner(mirror, "kz", bit_number)
    for bit_number in range(block_count.bit_length() - 1):
        mirror = from_partner(mirror, "ky", bit_number)
    signs = jnp.array([1.0, -1.0, 1.0], jnp.float32).reshape(3, 1, 1, 1)
    return half.astype(jnp.float32) + signs * mirror.astype(jnp.float32)


def solution(mesh):
    placed = (
        P("kz", "ky", None),
        P("kz", "ky", None),
        P("kz", "ky", None),
        P("kz", None),
        P("kz"),
        P("kz"),
        P("kz"),
        P(None, "kz"),
    )
    return jax.shard_map(
        per_device, mesh=mesh, in_specs=placed, out_specs=P(None, "kz", "ky", None), check_vma=False
    )
```

profile of v0, /device:TPU:1, one launch (start us, length us, event | category | flops | bytes accessed | tf_op | source)
XLA Modules:
  0.0 1078.8 jit_solution(6700450336136552983)
XLA Ops:
  7.2 8.4 all-to-all-start
  17.6 3.6 gather_fusion.2
  21.2 6.2 select_select_fusion
  27.5 7.2 all-to-all-start.1
  38.9 80.2 %all-to-all-done.1 = bf16[64,3,32,512]{3,2,1,0:T(8,128)(2,1)} async-done(((bf16[64,3,32,512]{3,2,1,0:T(8,128)(2,1)}), bf16[64,3,32,512]{3,2,1,0:T(8,128)(2,1)}, u32[]{:S(2)}, u32[]{:S(2)}) %all-to-all-start.1) | async-done | bytes 6291488 | tf_op jit(solution)/shard_map/all_to_all | solution.py:112
  119.0 6.3 gather_fusion.3
  125.4 6.1 broadcast_select_fusion
  131.4 5.4 broadcast_in_dim.120
  136.8 147.3 %while.16 = (s32[]{:T(128)}, f32[3,12,66,1024]{3,2,1,0:T(8,128)}, s32[]{:T(128)}, bf16[64,8]{1,0:T(8,128)(2,1)S(1)}, bf16[64,3,32,512]{3,2,1,0:T(8,128)(2,1)}, /...) while((s32[]{:T(128)}, f32[3,12,66,1024]{3,2,1,0:T(8,128)}, ...), condition=%wide.region_7.8_spmd.clone, body=%wide.region_6.7_spmd.clone.sunk | while | flops 3252840960 | bytes 125481800 | solution.py:158
  155.2 51.4 %fusion.95 = bf16[8,3,32,1024]{3,2,1,0:T(8,128)(2,1)S(1)} fusion(f32[8]{0:T(128)S(1)} %get-tuple-element.357, f32[512,1024]{1,0:T(8,128)S(1)} %fusion.94, bf16[64,3,32,512]{3,2,1,0:T(8,128)(2,1)} %get-tuple-element.395, s32[]{:T(128)S(6)} %select_n.122), kind=kOutput, calls=%fused_computation.26.clone.1 | convolution fusion | flops 1158414336 | bytes 4456484 | tf_op jit(solution)/shard_map/while/body/gcuv,gvx->gcux/dot_general | solution.py:60
  210.1 3.3 maximum_add_fusion.2
  213.4 4.0 copy-done
  221.9 51.4 %fusion.95 = bf16[8,3,32,1024]{3,2,1,0:T(8,128)(2,1)S(1)} fusion(f32[8]{0:T(128)S(1)} %get-tuple-element.357, f32[512,1024]{1,0:T(8,128)S(1)} %fusion.94, bf16[64,3,32,512]{3,2,1,0:T(8,128)(2,1)} %get-tuple-element.395, s32[]{:T(128)S(6)} %select_n.122), kind=kOutput, calls=%fused_computation.26.clone.1 | convolution fusion | flops 1158414336 | bytes 4456484 | tf_op jit(solution)/shard_map/while/body/gcuv,gvx->gcux/dot_general | solution.py:60
  280.1 4.0 copy-done
  284.2 3.8 fusion.76
  287.9 4.6 collective-permute-start
  294.4 36.5 %collective-permute-done = f32[3,4,66,1024]{3,2,1,0:T(8,128)S(1)} collective-permute-done((f32[3,4,66,1024]{3,2,1,0:T(8,128)S(1)}, f32[3,4,66,1024]{3,2,1,0:T(8,128)S(1)}, u32[]{:S(2)}, u32[]{:S(2)}) %collective-permute-start) | collective-permute-done | bytes 3244064 | tf_op jit(solution)/shard_map/ppermute | solution.py:22
  330.9 4.6 collective-permute-done.1
  335.5 3.3 fusion.75
  339.5 5.4 collective-permute-start.3
  348.9 5.9 rev.3
  354.7 3.6 collective-permute-done.4
  358.5 35.7 %collective-permute-done.5 = bf16[3,4,64,1024]{3,2,1,0:T(8,128)(2,1)S(1)} collective-permute-done((bf16[3,4,64,1024]{3,2,1,0:T(8,128)(2,1)S(1)}, bf16[3,4,64,1024]{3,2,1,0:T(8,128)(2,1)S(1)}, u32[]{:S(2)}, u32[]{:S(2)}) %collective-permute-start.5) | collective-permute-done | bytes 1572896 | tf_op jit(solution)/shard_map/ppermute | solution.py:32
  394.2 6.6 collective-permute-start.6
  400.8 34.1 %collective-permute-done.6 = bf16[3,4,64,1024]{3,2,1,0:T(8,128)(2,1)S(1)} collective-permute-done((bf16[3,4,64,1024]{3,2,1,0:T(8,128)(2,1)S(1)}, bf16[3,4,64,1024]{3,2,1,0:T(8,128)(2,1)S(1)}, u32[]{:S(2)}, u32[]{:S(2)}) %collective-permute-start.6) | collective-permute-done | bytes 1572896 | tf_op jit(solution)/shard_map/ppermute | solution.py:32
  434.9 396.6 %collective-permute-start.7 = (bf16[3,4,64,1024]{3,2,1,0:T(8,128)(2,1)S(1)}, bf16[3,4,64,1024]{3,2,1,0:T(8,128)(2,1)S(1)}, u32[]{:S(2)}, u32[]{:S(2)}) collective-permute-start(bf16[3,4,64,1024]{3,2,1,0:T(8,128)(2,1)S(1)} %collective-permute-done.6), channel_id=1, source_target_pairs={{0,128},{16,144},{32,160},{48,176},{64,192},{80,208},{96,224},{112... | collective-permute-start | bytes 4718600 | tf_op jit(solution)/shard_map/ppermute | solution.py:32
  831.5 32.8 %collective-permute-done.7 = bf16[3,4,64,1024]{3,2,1,0:T(8,128)(2,1)S(1)} collective-permute-done((bf16[3,4,64,1024]{3,2,1,0:T(8,128)(2,1)S(1)}, bf16[3,4,64,1024]{3,2,1,0:T(8,128)(2,1)S(1)}, u32[]{:S(2)}, u32[]{:S(2)}) %collective-permute-start.7) | collective-permute-done | bytes 1572896 | tf_op jit(solution)/shard_map/ppermute | solution.py:32
  864.3 33.3 %collective-permute-done.8 = bf16[3,4,64,1024]{3,2,1,0:T(8,128)(2,1)S(1)} collective-permute-done((bf16[3,4,64,1024]{3,2,1,0:T(8,128)(2,1)S(1)}, bf16[3,4,64,1024]{3,2,1,0:T(8,128)(2,1)S(1)}, u32[]{:S(2)}, u32[]{:S(2)}) %collective-permute-start.8) | collective-permute-done | bytes 1572896 | tf_op jit(solution)/shard_map/ppermute | solution.py:32
  897.7 32.4 %collective-permute-done.9 = bf16[3,4,64,1024]{3,2,1,0:T(8,128)(2,1)S(1)} collective-permute-done((bf16[3,4,64,1024]{3,2,1,0:T(8,128)(2,1)S(1)}, bf16[3,4,64,1024]{3,2,1,0:T(8,128)(2,1)S(1)}, u32[]{:S(2)}, u32[]{:S(2)}) %collective-permute-start.9) | collective-permute-done | bytes 1572896 | tf_op jit(solution)/shard_map/ppermute | solution.py:32
  930.1 5.2 collective-permute-start.10
  935.3 67.4 %collective-permute-done.10 = bf16[3,4,64,1024]{3,2,1,0:T(8,128)(2,1)S(1)} collective-permute-done((bf16[3,4,64,1024]{3,2,1,0:T(8,128)(2,1)S(1)}, bf16[3,4,64,1024]{3,2,1,0:T(8,128)(2,1)S(1)}, u32[]{:S(2)}, u32[]{:S(2)}) %collective-permute-start.10) | collective-permute-done | bytes 1572896 | tf_op jit(solution)/shard_map/ppermute | solution.py:32
  1004.7 71.5 %collective-permute-done.11 = bf16[3,4,64,1024]{3,2,1,0:T(8,128)(2,1)S(1)} collective-permute-done((bf16[3,4,64,1024]{3,2,1,0:T(8,128)(2,1)S(1)}, bf16[3,4,64,1024]{3,2,1,0:T(8,128)(2,1)S(1)}, u32[]{:S(2)}, u32[]{:S(2)}) %collective-permute-start.11) | collective-permute-done | bytes 1572896 | tf_op jit(solution)/shard_map/ppermute | solution.py:32
  (111 shorter events, 42.5 us)
Async XLA Ops:
  7.2 20.2 %all-to-all-start = ((bf16[16,4,8]{2,1,0:T(4,128)(2,1)}), bf16[16,4,8]{2,1,0:T(4,128)(2,1)S(1)}, u32[]{:S(2)}, u32[]{:S(2)}) async-start(bf16[16,4,8]{2,1,0:T(4,128)(2,1)} %select_select_fusion.1), calls=%async_computation | async-start | bytes 32768 | tf_op jit(solution)/shard_map/all_to_all | solution.py:113
  27.5 91.6 %all-to-all-start.1 = ((bf16[64,3,32,512]{3,2,1,0:T(8,128)(2,1)}), bf16[64,3,32,512]{3,2,1,0:T(8,128)(2,1)}, u32[]{:S(2)}, u32[]{:S(2)}) async-start(bf16[64,3,32,512]{3,2,1,0:T(8,128)(2,1)} %select_select_fusion), calls=%async_computation.1 | async-start | bytes 12582912 | tf_op jit(solution)/shard_map/all_to_all | solution.py:112
  153.4 56.7 %slice-start = ((s8[10616832]{0:T(1024)(128)(4,1)}), s8[4194304]{0:T(1024)(128)(4,1)S(1)}, s32[]{:S(2)}) async-start(s8[10616832]{0:T(1024)(128)(4,1)} %bitcast.74), calls=%async_computation.2 | async-start | bytes 8388608 | tf_op jit(solution)/shard_map/while
  155.2 54.9 %slice-start.1 = ((s8[10616832]{0:T(1024)(128)(4,1)}), s8[4194304]{0:T(1024)(128)(4,1)S(1)}, s32[]{:S(2)}) async-start(s8[10616832]{0:T(1024)(128)(4,1)} %bitcast.74), calls=%async_computation.3 | async-start | bytes 8388608 | tf_op jit(solution)/shard_map/while
  155.2 54.9 %slice-start.2 = ((s8[10616832]{0:T(1024)(128)(4,1)}), s8[2228224]{0:T(1024)(128)(4,1)S(1)}, s32[]{:S(2)}) async-start(s8[10616832]{0:T(1024)(128)(4,1)} %bitcast.74), calls=%async_computation.4 | async-start | bytes 4456448 | tf_op jit(solution)/shard_map/while
  213.4 4.0 copy-start
  220.1 56.7 %slice-start = ((s8[10616832]{0:T(1024)(128)(4,1)}), s8[4194304]{0:T(1024)(128)(4,1)S(1)}, s32[]{:S(2)}) async-start(s8[10616832]{0:T(1024)(128)(4,1)} %bitcast.74), calls=%async_computation.2 | async-start | bytes 8388608 | tf_op jit(solution)/shard_map/while
  221.9 54.9 %slice-start.1 = ((s8[10616832]{0:T(1024)(128)(4,1)}), s8[4194304]{0:T(1024)(128)(4,1)S(1)}, s32[]{:S(2)}) async-start(s8[10616832]{0:T(1024)(128)(4,1)} %bitcast.74), calls=%async_computation.3 | async-start | bytes 8388608 | tf_op jit(solution)/shard_map/while
  221.9 54.9 %slice-start.2 = ((s8[10616832]{0:T(1024)(128)(4,1)}), s8[2228224]{0:T(1024)(128)(4,1)S(1)}, s32[]{:S(2)}) async-start(s8[10616832]{0:T(1024)(128)(4,1)} %bitcast.74), calls=%async_computation.4 | async-start | bytes 4456448 | tf_op jit(solution)/shard_map/while
  280.1 4.0 copy-start
  287.9 43.0 %collective-permute-start = (f32[3,4,66,1024]{3,2,1,0:T(8,128)S(1)}, f32[3,4,66,1024]{3,2,1,0:T(8,128)S(1)}, u32[]{:S(2)}, u32[]{:S(2)}) collective-permute-start(f32[3,4,66,1024]{3,2,1,0:T(8,128)S(1)} %get-tuple-element.276), channel_id=1, source_target_pairs={{0,16},{16,32},{32,48},{48,64},{64,80},{80,96},{96,112},{112,128},... | collective-permute-start | bytes 9732104 | tf_op jit(solution)/shard_map/ppermute | solution.py:22
  292.5 43.0 %collective-permute-start.1 = (f32[3,4,66,1024]{3,2,1,0:T(8,128)S(1)}, f32[3,4,66,1024]{3,2,1,0:T(8,128)S(1)}, u32[]{:S(2)}, u32[]{:S(2)}) collective-permute-start(f32[3,4,66,1024]{3,2,1,0:T(8,128)S(1)} %get-tuple-element.277), channel_id=1, source_target_pairs={{16,0},{32,16},{48,32},{64,48},{80,64},{96,80},{112,96},{128,112},... | collective-permute-start | bytes 9732104 | tf_op jit(solution)/shard_map/ppermute | solution.py:22
  338.9 7.3 collective-permute-start.2
  339.5 7.4 collective-permute-start.3
  344.9 731.3 %copy-start.1 = (f32[3]{0:T(128)S(1)}, f32[3]{0:T(128)}, u32[]{:S(2)}) copy-start(f32[3]{0:T(128)} %constant.611.clone) | copy-start | bytes 40
  354.7 3.6 collective-permute-start.4
  358.4 35.9 %collective-permute-start.5 = (bf16[3,4,64,1024]{3,2,1,0:T(8,128)(2,1)S(1)}, bf16[3,4,64,1024]{3,2,1,0:T(8,128)(2,1)S(1)}, u32[]{:S(2)}, u32[]{:S(2)}) collective-permute-start(bf16[3,4,64,1024]{3,2,1,0:T(8,128)(2,1)S(1)} %collective-permute-done.4), channel_id=1, source_target_pairs={{0,32},{16,48},{32,0},{48,16},{64,96},{80,112},{96,64},{112,80},{1... | collective-permute-start | bytes 4718600 | tf_op jit(solution)/shard_map/ppermute | solution.py:32
  394.2 40.7 %collective-permute-start.6 = (bf16[3,4,64,1024]{3,2,1,0:T(8,128)(2,1)S(1)}, bf16[3,4,64,1024]{3,2,1,0:T(8,128)(2,1)S(1)}, u32[]{:S(2)}, u32[]{:S(2)}) collective-permute-start(bf16[3,4,64,1024]{3,2,1,0:T(8,128)(2,1)S(1)} %collective-permute-done.5), channel_id=1, source_target_pairs={{0,64},{16,80},{32,96},{48,112},{64,0},{80,16},{96,32},{112,48},{1... | collective-permute-start | bytes 4718600 | tf_op jit(solution)/shard_map/ppermute | solution.py:32
  434.9 429.4 %collective-permute-start.7 = (bf16[3,4,64,1024]{3,2,1,0:T(8,128)(2,1)S(1)}, bf16[3,4,64,1024]{3,2,1,0:T(8,128)(2,1)S(1)}, u32[]{:S(2)}, u32[]{:S(2)}) collective-permute-start(bf16[3,4,64,1024]{3,2,1,0:T(8,128)(2,1)S(1)} %collective-permute-done.6), channel_id=1, source_target_pairs={{0,128},{16,144},{32,160},{48,176},{64,192},{80,208},{96,224},{112... | collective-permute-start | bytes 4718600 | tf_op jit(solution)/shard_map/ppermute | solution.py:32
  864.3 33.3 %collective-permute-start.8 = (bf16[3,4,64,1024]{3,2,1,0:T(8,128)(2,1)S(1)}, bf16[3,4,64,1024]{3,2,1,0:T(8,128)(2,1)S(1)}, u32[]{:S(2)}, u32[]{:S(2)}) collective-permute-start(bf16[3,4,64,1024]{3,2,1,0:T(8,128)(2,1)S(1)} %collective-permute-done.7), channel_id=1, source_target_pairs={{0,1},{1,0},{2,3},{3,2},{4,5},{5,4},{6,7},{7,6},{8,9},{9,8},{10,11... | collective-permute-start | bytes 4718600 | tf_op jit(solution)/shard_map/ppermute | solution.py:32
  897.7 32.4 %collective-permute-start.9 = (bf16[3,4,64,1024]{3,2,1,0:T(8,128)(2,1)S(1)}, bf16[3,4,64,1024]{3,2,1,0:T(8,128)(2,1)S(1)}, u32[]{:S(2)}, u32[]{:S(2)}) collective-permute-start(bf16[3,4,64,1024]{3,2,1,0:T(8,128)(2,1)S(1)} %collective-permute-done.8), channel_id=1, source_target_pairs={{0,2},{1,3},{2,0},{3,1},{4,6},{5,7},{6,4},{7,5},{8,10},{9,11},{10,... | collective-permute-start | bytes 4718600 | tf_op jit(solution)/shard_map/ppermute | solution.py:32
  930.1 72.6 %collective-permute-start.10 = (bf16[3,4,64,1024]{3,2,1,0:T(8,128)(2,1)S(1)}, bf16[3,4,64,1024]{3,2,1,0:T(8,128)(2,1)S(1)}, u32[]{:S(2)}, u32[]{:S(2)}) collective-permute-start(bf16[3,4,64,1024]{3,2,1,0:T(8,128)(2,1)S(1)} %collective-permute-done.9), channel_id=1, source_target_pairs={{0,4},{1,5},{2,6},{3,7},{4,0},{5,1},{6,2},{7,3},{8,12},{9,13},{10,... | collective-permute-start | bytes 4718600 | tf_op jit(solution)/shard_map/ppermute | solution.py:32
  1002.7 73.5 %collective-permute-start.11 = (bf16[3,4,64,1024]{3,2,1,0:T(8,128)(2,1)S(1)}, bf16[3,4,64,1024]{3,2,1,0:T(8,128)(2,1)S(1)}, u32[]{:S(2)}, u32[]{:S(2)}) collective-permute-start(bf16[3,4,64,1024]{3,2,1,0:T(8,128)(2,1)S(1)} %collective-permute-done.10), channel_id=1, source_target_pairs={{0,8},{1,9},{2,10},{3,11},{4,12},{5,13},{6,14},{7,15},{8,0},{9,1},... | collective-permute-start | bytes 4718600 | tf_op jit(solution)/shard_map/ppermute | solution.py:32
where the time goes:
time: 1080 us
  starting transfers between devices  439 us (41%)
  waiting for transfers between devices  433 us (40%)
  matrix products  110 us (10%)
  other arithmetic  43.7 us (4%)
  local copies, waits for them, and re-layouts  38.2 us (4%)
  loops' own time  14.2 us (1%)
    ppermute x8, starting transfers between devices, from_partner(): lax.ppermute(shard, axis, [(i, i ^ 1 << distance) for i in range(lax.axis...  411 us
    ppermute x8, waiting for transfers between devices, from_partner(): lax.ppermute(shard, axis, [(i, i ^ 1 << distance) for i in range(lax.axis...  311 us
    dot_general x2, matrix products, spread_x(): jnp.einsum('gcuv,gvx->gcux', portion, table, preferred_element_type=jnp.f...  103 us
    all_to_all x1, waiting for transfers between devices, per_device(): lax.all_to_all(to_slots(data), 'kz', split_axis=0, concat_axis=0, tiled=T...  80.2 us
    ppermute x2, waiting for transfers between devices, passed_along(): return lax.ppermute(shard, axis, pairs)  41.1 us
  transfers between devices with their start and end apart: 14, of which 12 were waited for; matrix products, arithmetic and copies ran while one was open for 2% of the time, Pallas kernels for 0%

commit v1 on v0

v1 whole, which is shorter than its diff:
```python
import functools
import math

import jax
import jax.numpy as jnp
from jax import lax
from jax.experimental import pallas as pl
from jax.experimental.pallas import tpu as pltpu
from jax.sharding import PartitionSpec as P

ZD = 4
MZ = 4
ZE = 12
CAP = 4
SLABS = 16
SLOTS = SLABS * CAP
SLICE = 512
GRID = 1024
STRIP = 32
LINES = 64
HALF = 16
KC = SLOTS * HALF
MAIN = ZE * 32
MROWS = MAIN + 32

kernel_beta = 7.4
kernel_reach = 2.0
twist_step = 0.37

MESH = pl.DeviceIdType.MESH


def series(quarter):
    total = jnp.full_like(quarter, 1.0 / math.factorial(25) ** 2)
    for order in range(24, 0, -1):
        total = total * quarter + 1.0 / math.factorial(order) ** 2
    return total * quarter


SCALE = sum((kernel_beta * kernel_beta / 4) ** m / math.factorial(m) ** 2 for m in range(1, 26))


def kaiser(distance):
    inside = jnp.maximum(1.0 - distance * distance * 0.25, 0.0)
    return series(inside * (kernel_beta * kernel_beta * 0.25)) * (1.0 / SCALE)


def insert_kernel(w_ref, g_ref, cs_ref, pay_ref, mid_ref, up_ref, dn_ref, halo_ref, bc, bw, ac, aw):
    row_index = lax.axis_index("ky")

    @pl.loop(0, SLOTS)
    def _(n):
        wa, wb, wc, wd = w_ref[n, 0], w_ref[n, 1], w_ref[n, 2], w_ref[n, 3]
        for c in range(3):
            d = pay_ref[n, c].astype(jnp.float32)
            before = pltpu.roll(d, 1, 1)
            after = pltpu.roll(d, SLICE - 1, 1)
            even = (wa * d + wb * before).astype(jnp.bfloat16)
            odd = (wc * d + wd * after).astype(jnp.bfloat16)
            for q in range(2):
                if c < 2:
                    rows = pl.ds(pl.multiple_of(c * KC + n * HALF, HALF), HALF)
                    target = bc
                else:
                    rows = pl.ds(pl.multiple_of(n * HALF, HALF), HALF)
                    target = bw
                target[q, rows, 0:SLICE] = even[q * HALF : (q + 1) * HALF]
                target[q, rows, SLICE:GRID] = odd[q * HALF : (q + 1) * HALF]

    plane, live, tilt, shift = g_ref[0:1], g_ref[2:3], g_ref[3:4], g_ref[4:5]
    local = lax.broadcasted_iota(jnp.int32, (1, KC), 1) % HALF
    level = (lax.broadcasted_iota(jnp.int32, (16, 1), 0) - MZ).astype(jnp.float32)
    line = lax.broadcasted_iota(jnp.int32, (32, 1), 0)
    main_y = kaiser((line - 2 * local).astype(jnp.float32) - shift)
    low_y = kaiser((-1 - 2 * local).astype(jnp.float32) - shift)
    high_y = kaiser((32 - 2 * local).astype(jnp.float32) - shift)
    for q in range(2):
        row = row_index * STRIP + q * HALF + local - SLICE // 2
        centre = plane + tilt * row.astype(jnp.float32) / (SLICE // 2)
        along = kaiser(level - centre) * live
        real, imag = along * cs_ref[0:16], along * cs_ref[16:32]
        for part, value_y in ((0, low_y), (16, high_y)):
            rows = slice(MAIN + part, MAIN + part + 16)
            again = slice(MROWS + MAIN + part, MROWS + MAIN + part + 16)
            kr = (real * value_y).astype(jnp.bfloat16)
            ki = imag * value_y
            ac[q, rows, 0:KC] = kr
            ac[q, rows, KC : 2 * KC] = (-ki).astype(jnp.bfloat16)
            ac[q, again, 0:KC] = ki.astype(jnp.bfloat16)
            ac[q, again, KC : 2 * KC] = kr
            aw[q, rows, :] = (along * value_y).astype(jnp.bfloat16)
        for z in range(ZE):
            rows = slice(z * 32, z * 32 + 32)
            again = slice(MROWS + z * 32, MROWS + z * 32 + 32)
            kr = (real[z : z + 1] * main_y).astype(jnp.bfloat16)
            ki = imag[z : z + 1] * main_y
            ac[q, rows, 0:KC] = kr
            ac[q, rows, KC : 2 * KC] = (-ki).astype(jnp.bfloat16)
            ac[q, again, 0:KC] = ki.astype(jnp.bfloat16)
            ac[q, again, KC : 2 * KC] = kr
            aw[q, rows, :] = (along[z : z + 1] * main_y).astype(jnp.bfloat16)

    lines = lax.broadcasted_iota(jnp.int32, (1, 32, 1), 1)

    @pl.loop(0, GRID // 256)
    def _(tile):
        cols = pl.ds(pl.multiple_of(tile * 256, 256), 256)
        for c in range(3):
            if c < 2:
                parts = [
                    jnp.dot(
                        ac[q, c * MROWS : (c + 1) * MROWS, :],
                        bc[q, :, cols],
                        preferred_element_type=jnp.float32,
                    )
                    for q in range(2)
                ]
            else:
                parts = [
                    jnp.dot(aw[q], bw[q, :, cols], preferred_element_type=jnp.float32)
                    for q in range(2)
                ]
            low = [part[MAIN : MAIN + ZE] for part in parts]
            high = [part[MAIN + 16 : MAIN + 16 + ZE] for part in parts]
            main = [part[:MAIN].reshape(ZE, 32, 256) for part in parts]
            main[0] = main[0] + jnp.where(lines == 31, low[1][:, None, :], 0.0)
            main[1] = main[1] + jnp.where(lines == 0, high[0][:, None, :], 0.0)
            for q in range(2):
                span = slice(q * 32, q * 32 + 32)
                dn_ref[c, :, span, cols] = main[q][0:MZ].astype(jnp.bfloat16)
                mid_ref[c, :, span, cols] = main[q][MZ : MZ + ZD]
                up_ref[c, :, span, cols] = main[q][MZ + ZD :].astype(jnp.bfloat16)
            for j in range(3):
                halo_ref[j, c * ZD : (c + 1) * ZD, cols] = low[0][j * 4 : j * 4 + 4]
                halo_ref[3 + j, c * ZD : (c + 1) * ZD, cols] = high[1][j * 4 : j * 4 + 4]


def insert(weights, geometry, phases, payload):
    vmem = pl.BlockSpec(memory_space=pltpu.VMEM)
    return pl.pallas_call(
        insert_kernel,
        out_shape=(
            jax.ShapeDtypeStruct((3, ZD, LINES, GRID), jnp.float32),
            jax.ShapeDtypeStruct((3, ZD, LINES, GRID), jnp.bfloat16),
            jax.ShapeDtypeStruct((3, ZD, LINES, GRID), jnp.bfloat16),
            jax.ShapeDtypeStruct((6, 16, GRID), jnp.float32),
        ),
        in_specs=[pl.BlockSpec(memory_space=pltpu.SMEM), vmem, vmem, vmem],
        out_specs=(vmem, vmem, vmem, vmem),
        scratch_shapes=[
            pltpu.VMEM((2, 2 * KC, GRID), jnp.bfloat16),
            pltpu.VMEM((2, KC, GRID), jnp.bfloat16),
            pltpu.VMEM((2, 2 * MROWS, 2 * KC), jnp.bfloat16),
            pltpu.VMEM((2, MROWS, KC), jnp.bfloat16),
        ],
        compiler_params=pltpu.CompilerParams(vmem_limit_bytes=60 << 20),
        name="insert",
    )(weights, geometry, phases, payload)


def exchange_kernel(
    mid_ref, up_ref, dn_ref, halo_ref, out_ref,
    from_low, from_high, halos, half, mirror, perm, back, send, recv,
):
    kz, ky = lax.axis_index("kz"), lax.axis_index("ky")
    above, below = lax.rem(kz + 1, 16), lax.rem(kz + 15, 16)
    after, before = lax.rem(ky + 1, 16), lax.rem(ky + 15, 16)
    partner = {"kz": 15 - kz, "ky": 15 - ky}
    slabs = (below, kz, above)
    peers = [{"kz": above, "ky": ky}, {"kz": below, "ky": ky}]
    peers += [{"kz": s, "ky": r} for s in slabs for r in (before, after)]
    peers += [partner]
    barrier = pltpu.get_barrier_semaphore()
    for peer in peers:
        pl.semaphore_signal(barrier, inc=1, device_id=peer, device_id_type=MESH)
    pl.semaphore_wait(barrier, len(peers))

    def copy(source, target, number, peer):
        return pltpu.make_async_remote_copy(
            src_ref=source, dst_ref=target, send_sem=send.at[number], recv_sem=recv.at[number],
            device_id=peer, device_id_type=MESH,
        )

    first = [copy(up_ref, from_low, 0, peers[0]), copy(dn_ref, from_high, 1, peers[1])]
    for j in range(3):
        for side, target in ((0, before), (1, after)):
            number = side * 3 + j
            first.append(
                copy(
                    halo_ref.at[number], halos.at[number], 2 + number,
                    {"kz": slabs[j], "ky": target},
                )
            )
    for item in first:
        item.start()

    @pl.loop(0, GRID // 128)
    def _(tile):
        rows = pl.multiple_of(tile * 128, 128)
        k = lax.broadcasted_iota(jnp.int32, (128, GRID), 0) + rows
        x = lax.broadcasted_iota(jnp.int32, (128, GRID), 1)
        wanted = jnp.where(k < SLICE, 2 * k, 2 * (k - SLICE) + 1)
        perm[pl.ds(rows, 128), :] = (x == wanted).astype(jnp.float32).astype(jnp.bfloat16)
        back[pl.ds(rows, 128), :] = (GRID - 1 - x == wanted).astype(jnp.float32).astype(jnp.bfloat16)

    for item in first:
        item.wait()

    lower = jnp.where(kz > 0, 1.0, 0.0)
    upper = jnp.where(kz < 15, 1.0, 0.0)
    lines = lax.broadcasted_iota(jnp.int32, (LINES, 1), 0)
    copies = []
    for c in range(3):

        @pl.loop(0, ZD)
        def _(p):
            row = pl.ds(c * ZD + p, 1)
            total = mid_ref[c, p] + lower * from_low[c, p].astype(jnp.float32)
            total = total + upper * from_high[c, p].astype(jnp.float32)
            last = upper * halos[0, row, :] + halos[1, row, :] + lower * halos[2, row, :]
            start = upper * halos[3, row, :] + halos[4, row, :] + lower * halos[5, row, :]
            total = total + jnp.where(lines == LINES - 1, last, 0.0)
            total = total + jnp.where(lines == 0, start, 0.0)
            half[c, pl.ds(pl.multiple_of(p * LINES, LINES), LINES), :] = total.astype(jnp.bfloat16)

        item = copy(half.at[c], mirror.at[c], 8 + c, partner)
        item.start()
        copies.append(item)

    for c in range(3):

        @pl.loop(0, GRID // 256)
        def _(tile):
            cols = pl.ds(pl.multiple_of(tile * 256, 256), 256)
            out_ref[c, :, cols] = jnp.dot(
                half[c], perm[:, cols], preferred_element_type=jnp.float32
            )

    i = lax.broadcasted_iota(jnp.int32, (256, 256), 0)
    j = lax.broadcasted_iota(jnp.int32, (256, 256), 1)
    flip = (i + j == 255).astype(jnp.float32).astype(jnp.bfloat16)
    for c, sign in ((0, 1.0), (1, -1.0), (2, 1.0)):
        copies[c].wait()
        turned = jnp.dot(flip, mirror[c], preferred_element_type=jnp.float32)
        mirror[c] = turned.astype(jnp.bfloat16)

        @pl.loop(0, GRID // 256)
        def _(tile):
            cols = pl.ds(pl.multiple_of(tile * 256, 256), 256)
            out_ref[c, :, cols] += sign * jnp.dot(
                mirror[c], back[:, cols], preferred_element_type=jnp.float32
            )


def exchange(mid, up, dn, halo):
    vmem = pl.BlockSpec(memory_space=pltpu.VMEM)
    return pl.pallas_call(
        exchange_kernel,
        out_shape=jax.ShapeDtypeStruct((3, ZD * LINES, GRID), jnp.float32),
        in_specs=[vmem] * 4,
        out_specs=vmem,
        scratch_shapes=[
            pltpu.VMEM((3, ZD, LINES, GRID), jnp.bfloat16),
            pltpu.VMEM((3, ZD, LINES, GRID), jnp.bfloat16),
            pltpu.VMEM((6, 16, GRID), jnp.float32),
            pltpu.VMEM((3, ZD * LINES, GRID), jnp.bfloat16),
            pltpu.VMEM((3, ZD * LINES, GRID), jnp.bfloat16),
            pltpu.VMEM((GRID, GRID), jnp.bfloat16),
            pltpu.VMEM((GRID, GRID), jnp.bfloat16),
            pltpu.SemaphoreType.DMA((11,)),
            pltpu.SemaphoreType.DMA((11,)),
        ],
        compiler_params=pltpu.CompilerParams(
            collective_id=1, has_side_effects=True, vmem_limit_bytes=60 << 20
        ),
        name="exchange",
    )(mid, up, dn, halo)


def per_device(
    slice_re, slice_im, slice_ctf, slice_dest, slice_plane, helix_index, slice_tilt, slice_shift
):
    slab_index = lax.axis_index("kz")
    held_count = slice_re.shape[0]
    ctf = slice_ctf.astype(jnp.float32)
    data = jnp.stack(
        [ctf * slice_re.astype(jnp.float32), ctf * slice_im.astype(jnp.float32), ctf * ctf], axis=1
    ).astype(jnp.bfloat16)
    ones = jnp.ones((held_count,), jnp.float32)
    zeros = jnp.zeros((held_count,), jnp.float32)
    geometry = jnp.stack(
        [
            slice_plane.astype(jnp.float32),
            helix_index.astype(jnp.float32),
            ones,
            slice_tilt.astype(jnp.float32),
            slice_shift[0].astype(jnp.float32),
            slice_shift[1].astype(jnp.float32),
            zeros,
            zeros,
        ],
        axis=1,
    ).astype(jnp.bfloat16)
    target = slice_dest[:, 0]
    onehot = (target[:, None] == jnp.arange(SLABS)[None, :]).astype(jnp.int32)
    ranking = jnp.sum((jnp.cumsum(onehot, axis=0) - 1) * onehot, axis=1)
    position = target * CAP + ranking
    matches = (jnp.arange(SLOTS)[:, None] == position[None, :]).astype(jnp.int32)
    occupied = jnp.sum(matches, axis=1) > 0
    source_row = jnp.sum(matches * jnp.arange(held_count)[None, :], axis=1)
    payload = lax.all_to_all(
        jnp.take(data, source_row, axis=0), "kz", split_axis=0, concat_axis=0, tiled=True
    )
    slots = jnp.where(occupied[:, None], jnp.take(geometry, source_row, axis=0), 0)
    arrived = lax.all_to_all(slots, "kz", split_axis=0, concat_axis=0, tiled=True)
    arrived = arrived.astype(jnp.float32)
    offset = arrived[:, 5:6]
    weights = kaiser(jnp.array([[0.0, 2.0, 1.0, -1.0]]) - offset)
    weights = weights.astype(jnp.bfloat16).astype(jnp.float32)
    band = slab_index * ZD + jnp.arange(16) - MZ
    angle = twist_step * (arrived[:, 1].astype(jnp.int32)[None, :] * band[:, None]).astype(
        jnp.float32
    )
    phases = jnp.repeat(jnp.concatenate([jnp.cos(angle), jnp.sin(angle)], axis=0), HALF, axis=1)
    spread = jnp.repeat(arrived.T, HALF, axis=1)
    mid, up, dn, halo = insert(weights, spread, phases, payload)
    out = exchange(mid, up, dn, halo)
    return out.reshape(3, ZD, LINES, GRID)


def solution(mesh):
    placed = (
        P("kz", "ky", None),
        P("kz", "ky", None),
        P("kz", "ky", None),
        P("kz", None),
        P("kz"),
        P("kz"),
        P("kz"),
        P(None, "kz"),
    )
    return jax.shard_map(
        per_device, mesh=mesh, in_specs=placed, out_specs=P(None, "kz", "ky", None), check_vma=False
    )
```

time: 1080 us -> 261 us (0.24)
  starting transfers between devices: 439 us -> 15.8 us
  waiting for transfers between devices: 433 us -> 81.2 us
  Pallas kernels: 0 us -> 137 us
  matrix products: 110 us -> 0 us
  other arithmetic: 43.7 us -> 13.5 us
  local copies, waits for them, and re-layouts: 38.2 us -> 12.4 us
  loops' own time: 14.2 us -> 0 us
    ppermute x12 -> x0, starting transfers between devices: 423 us -> none  [the longest x8 411 us: from_partner(): lax.ppermute(shard, axis, [(i, i ^ 1 << distance) for i in range(lax.axis...]
    ppermute x12 -> x0, waiting for transfers between devices: 353 us -> none  [the longest x8 311 us: from_partner(): lax.ppermute(shard, axis, [(i, i ^ 1 << distance) for i in range(lax.axis...]
    pallas_call x0 -> x2, Pallas kernels: none -> 137 us  [the longest x1 111 us: exchange(): pl.pallas_call(exchange_kernel, out_shape=jax.ShapeDtypeStruct((3, ZD * L...]
    dot_general x6 -> x0, matrix products: 110 us -> none  [the longest x2 103 us: spread_x(): jnp.einsum('gcuv,gvx->gcux', portion, table, preferred_element_type=jnp.f...]
    another operation x1 -> x0, loops' own time: 14.2 us -> none  [per_device(): volume = lax.fori_loop(0, block_total, spread_block, volume)]
  transfers between devices with their start and end apart: 14 -> 2, of which waited for: 12 -> 1; matrix products, arithmetic and copies ran while one was open for 2% -> 6% of each run, Pallas kernels for 0% -> 0%
where the time goes in v1:
time: 261 us; the launch traced here: 260 us
  Pallas kernels  137 us (52%)
  waiting for transfers between devices  81.2 us (31%)
  starting transfers between devices  15.8 us (6%)
  other arithmetic  13.5 us (5%)
  local copies, waits for them, and re-layouts  12.4 us (5%)
    pallas_call x1, Pallas kernels, exchange(): pl.pallas_call(exchange_kernel, out_shape=jax.ShapeDtypeStruct((3, ZD * L...  111 us
    all_to_all x1, waiting for transfers between devices, per_device(): lax.all_to_all(jnp.take(data, source_row, axis=0), 'kz', split_axis=0, co...  81.2 us
    pallas_call x1, Pallas kernels, insert(): pl.pallas_call(insert_kernel, out_shape=(jax.ShapeDtypeStruct((3, ZD, LIN...  25.9 us
    all_to_all x1, starting transfers between devices, per_device(): lax.all_to_all(slots, 'kz', split_axis=0, concat_axis=0, tiled=True)  8.45 us
    all_to_all x1, starting transfers between devices, per_device(): lax.all_to_all(jnp.take(data, source_row, axis=0), 'kz', split_axis=0, co...  7.36 us
    select_n x1, other arithmetic, per_device(): jnp.take(data, source_row, axis=0)  6.11 us
  transfers between devices with their start and end apart: 2, of which 1 were waited for; matrix products, arithmetic and copies ran while one was open for 6% of the time, Pallas kernels for 0%

profile of v1, /device:TPU:1, one launch (start us, length us, event | category | flops | bytes accessed | tf_op | source)
XLA Modules:
  0.0 260.3 jit_solution(7469191403277711660)
XLA Ops:
  0.0 0.7 fusion.10
  0.8 0.8 select_reduce_fusion.1
  1.6 0.7 multiply_add_fusion
  2.4 0.7 convert_bitcast_fusion.2
  3.1 0.7 convert_bitcast_fusion.1
  3.8 0.7 slice_bitcast_fusion
  4.5 0.1 copy.41
  4.6 0.1 copy.38
  4.7 0.1 copy.37
  4.8 0.1 copy.40
  4.9 0.8 copy.39
  5.6 0.1 gt.19
  5.8 0.1 stack.41
  5.9 0.6 gather_fusion
  6.5 0.7 select_select_fusion
  7.2 8.4 %all-to-all-start = ((bf16[16,4,8]{2,1,0:T(4,128)(2,1)}), bf16[16,4,8]{2,1,0:T(4,128)(2,1)S(1)}, u32[]{:S(2)}, u32[]{:S(2)}) async-start(bf16[16,4,8]{2,1,0:T(4,128)(2,1)} %select_select_fusion), calls=%async_computation | async-start | bytes 32768 | tf_op jit(solution)/shard_map/all_to_all | solution.py:315
  15.7 1.8 fusion.5
  17.5 0.2 pad_maximum_fusion
  17.6 3.6 %gather_fusion.1 = bf16[64,3,32,512]{3,2,1,0:T(8,128)(2,1)} fusion(bf16[16,3,32,512]{3,2,0,1:T(8,128)(2,1)S(1)} %pad_maximum_fusion, s32[1024]{0:T(1024)S(1)} %pad_clamp_fusion), kind=kCustom, calls=%fused_computation.1 | custom fusion | bytes 12583168 | tf_op jit(solution)/shard_map/jit(_take)/gather | solution.py:312
  21.2 6.1 %broadcast_select_fusion = bf16[64,3,32,512]{3,2,1,0:T(8,128)(2,1)} fusion(bf16[64,3,32,512]{3,2,1,0:T(8,128)(2,1)} %gather_fusion.1, pred[64]{0:T(512)(128)(4,1)S(1)} %compare_and_fusion.1), kind=kLoop, calls=%fused_computation.2 | loop fusion | flops 3145728 | bytes 12582976 | tf_op jit(solution)/shard_map/jit(_take)/select_n | solution.py:312
  27.4 7.4 %all-to-all-start.1 = ((bf16[64,3,32,512]{3,2,1,0:T(8,128)(2,1)}), bf16[64,3,32,512]{3,2,1,0:T(8,128)(2,1)}, u32[]{:S(2)}, u32[]{:S(2)}) async-start(bf16[64,3,32,512]{3,2,1,0:T(8,128)(2,1)} %broadcast_select_fusion), calls=%async_computation.1 | async-start | bytes 12582912 | tf_op jit(solution)/shard_map/all_to_all | solution.py:311
  34.7 0.2 fusion.6
  34.9 0.1 fusion.9
  35.2 0.1 broadcast_in_dim.49
  35.3 0.8 reshape.91.g_ref
  36.2 0.8 copy.46.cs_ref
  37.0 0.2 slice_reduce_fusion
  37.2 0.7 fusion.7.w_ref
  37.9 81.2 %all-to-all-done.1.pay_ref = bf16[64,3,32,512]{3,2,1,0:T(8,128)(2,1)} async-done(((bf16[64,3,32,512]{3,2,1,0:T(8,128)(2,1)}), bf16[64,3,32,512]{3,2,1,0:T(8,128)(2,1)}, u32[]{:S(2)}, u32[]{:S(2)}) %all-to-all-start.1) | async-done | bytes 6291488 | tf_op jit(solution)/shard_map/all_to_all | solution.py:311
  119.1 25.9 %insert.1 = (f32[3,4,64,1024]{3,2,1,0:T(8,128)}, bf16[3,4,64,1024]{3,2,1,0:T(8,128)(2,1)}, bf16[3,4,64,1024]{3,2,1,0:T(8,128)(2,1)}, f32[6,16,1024]{2,1,0:T(8,128)}) custom-call(f32[64,4]{1,0:T(8,128)} %fusion.7.w_ref, f32[8,1024]{1,0:T(8,128)} %reshape.91.g_ref, f32[32,1024]{1,0:T(8,128)} %copy.46.cs_ref, bf16[64,3,32,512]{3,2,1,0:T(8,128)(2,1)} %all-to-all-done.1.pay_ref), custom_call_target="tpu_custom_call" | custom-call | tf_op jit(solution)/shard_map/insert/pallas_call | solution.py:140
  145.0 111.3 %exchange.1 = f32[3,256,1024]{2,1,0:T(8,128)} custom-call(f32[3,4,64,1024]{3,2,1,0:T(8,128)} %get-tuple-element.9.mid_ref, bf16[3,4,64,1024]{3,2,1,0:T(8,128)(2,1)} %get-tuple-element.10.up_ref, bf16[3,4,64,1024]{3,2,1,0:T(8,128)(2,1)} %get-tuple-element.11.dn_ref, f32[6,16,1024]{2,1,0:T(8,128)} %get-tuple-element.12.halo_ref), custom_call_target="tpu_custom_call" | custom-call | tf_op jit(solution)/shard_map/exchange/pallas_call | solution.py:257
  256.4 4.0 %copy.48 = f32[3,4,64,1024]{3,2,1,0:T(8,128)} copy(f32[3,4,64,1024]{3,2,1,0:T(8,128)} %bitcast.28) | data formatting | bytes 6291456
  (20 shorter events, 0.4 us)
Async XLA Ops:
  7.2 20.1 %all-to-all-start = ((bf16[16,4,8]{2,1,0:T(4,128)(2,1)}), bf16[16,4,8]{2,1,0:T(4,128)(2,1)S(1)}, u32[]{:S(2)}, u32[]{:S(2)}) async-start(bf16[16,4,8]{2,1,0:T(4,128)(2,1)} %select_select_fusion), calls=%async_computation | async-start | bytes 32768 | tf_op jit(solution)/shard_map/all_to_all | solution.py:315
  27.3 9.8 %copy-start = (f32[4]{0:T(128)S(1)}, f32[4]{0:T(128)}, u32[]{:S(2)}) copy-start(f32[4]{0:T(128)} %constant.113) | copy-start | bytes 52
  27.4 91.7 %all-to-all-start.1 = ((bf16[64,3,32,512]{3,2,1,0:T(8,128)(2,1)}), bf16[64,3,32,512]{3,2,1,0:T(8,128)(2,1)}, u32[]{:S(2)}, u32[]{:S(2)}) async-start(bf16[64,3,32,512]{3,2,1,0:T(8,128)(2,1)} %broadcast_select_fusion), calls=%async_computation.1 | async-start | bytes 12582912 | tf_op jit(solution)/shard_map/all_to_all | solution.py:311

commit v2 on v1

v2 whole, which is shorter than its diff:
```python
import functools
import math

import jax
import jax.numpy as jnp
from jax import lax
from jax.experimental import pallas as pl
from jax.experimental.pallas import tpu as pltpu
from jax.sharding import PartitionSpec as P

ZD = 4
MZ = 4
ZE = 12
CAP = 4
SLABS = 16
SLOTS = SLABS * CAP
SLICE = 512
GRID = 1024
SPARE = 4
ALL = SLABS * (1 + SPARE)
KA = ALL * 16
STRIP = 32
LINES = 64
HALF = 16
KC = SLOTS * HALF
MAIN = ZE * 32
MROWS = MAIN + 32

kernel_beta = 7.4
kernel_reach = 2.0
twist_step = 0.37

MESH = pl.DeviceIdType.MESH


def series(quarter):
    total = jnp.full_like(quarter, 1.0 / math.factorial(25) ** 2)
    for order in range(24, 0, -1):
        total = total * quarter + 1.0 / math.factorial(order) ** 2
    return total * quarter


SCALE = sum((kernel_beta * kernel_beta / 4) ** m / math.factorial(m) ** 2 for m in range(1, 26))


def kaiser(distance):
    inside = jnp.maximum(1.0 - distance * distance * 0.25, 0.0)
    return series(inside * (kernel_beta * kernel_beta * 0.25)) * (1.0 / SCALE)


def insert_kernel(count, w_ref, g_ref, cs_ref, pay_ref, mid_ref, up_ref, dn_ref, halo_ref, b, a):
    row_index = lax.axis_index("ky")

    @pl.loop(0, SLOTS)
    def _(n):
        wa, wb, wc, wd = w_ref[n, 0], w_ref[n, 1], w_ref[n, 2], w_ref[n, 3]
        for c in range(count):
            d = pay_ref[n, c].astype(jnp.float32)
            before = pltpu.roll(d, 1, 1)
            after = pltpu.roll(d, SLICE - 1, 1)
            even = (wa * d + wb * before).astype(jnp.bfloat16)
            odd = (wc * d + wd * after).astype(jnp.bfloat16)
            rows = pl.ds(pl.multiple_of(c * KC + n * HALF, HALF), HALF)
            for q in range(2):
                b[q, rows, 0:SLICE] = even[q * HALF : (q + 1) * HALF]
                b[q, rows, SLICE:GRID] = odd[q * HALF : (q + 1) * HALF]

    plane, live, tilt, shift = g_ref[0:1], g_ref[2:3], g_ref[3:4], g_ref[4:5]
    local = lax.broadcasted_iota(jnp.int32, (1, KC), 1) % HALF
    level = (lax.broadcasted_iota(jnp.int32, (16, 1), 0) - MZ).astype(jnp.float32)
    line = lax.broadcasted_iota(jnp.int32, (32, 1), 0)
    main_y = kaiser((line - 2 * local).astype(jnp.float32) - shift)
    low_y = kaiser((-1 - 2 * local).astype(jnp.float32) - shift)
    high_y = kaiser((32 - 2 * local).astype(jnp.float32) - shift)
    for q in range(2):
        row = row_index * STRIP + q * HALF + local - SLICE // 2
        centre = plane + tilt * row.astype(jnp.float32) / (SLICE // 2)
        along = kaiser(level - centre) * live
        parts = [(MAIN, slice(0, 16), low_y), (MAIN + 16, slice(0, 16), high_y)]
        parts += [(z * 32, slice(z, z + 1), main_y) for z in range(ZE)]
        if count == 2:
            real, imag = along * cs_ref[0:16], along * cs_ref[16:32]
        for first, levels, value_y in parts:
            size = 16 if first >= MAIN else 32
            rows = slice(first, first + size)
            again = slice(MROWS + first, MROWS + first + size)
            if count == 2:
                kr = (real[levels] * value_y).astype(jnp.bfloat16)
                ki = imag[levels] * value_y
                a[q, rows, 0:KC] = kr
                a[q, rows, KC : 2 * KC] = (-ki).astype(jnp.bfloat16)
                a[q, again, 0:KC] = ki.astype(jnp.bfloat16)
                a[q, again, KC : 2 * KC] = kr
            else:
                a[q, rows, :] = (along[levels] * value_y).astype(jnp.bfloat16)

    lines = lax.broadcasted_iota(jnp.int32, (1, 32, 1), 1)

    @pl.loop(0, GRID // 256)
    def _(tile):
        cols = pl.ds(pl.multiple_of(tile * 256, 256), 256)
        for c in range(count):
            parts = [
                jnp.dot(
                    a[q, c * MROWS : (c + 1) * MROWS, :],
                    b[q, :, cols],
                    preferred_element_type=jnp.float32,
                )
                for q in range(2)
            ]
            low = [part[MAIN : MAIN + ZE] for part in parts]
            high = [part[MAIN + 16 : MAIN + 16 + ZE] for part in parts]
            main = [part[:MAIN].reshape(ZE, 32, 256) for part in parts]
            main[0] = main[0] + jnp.where(lines == 31, low[1][:, None, :], 0.0)
            main[1] = main[1] + jnp.where(lines == 0, high[0][:, None, :], 0.0)
            for q in range(2):
                span = slice(q * 32, q * 32 + 32)
                dn_ref[c, :, span, cols] = main[q][0:MZ].astype(jnp.bfloat16)
                mid_ref[c, :, span, cols] = main[q][MZ : MZ + ZD]
                up_ref[c, :, span, cols] = main[q][MZ + ZD :].astype(jnp.bfloat16)
            for j in range(3):
                halo_ref[j, c * ZD : (c + 1) * ZD, cols] = low[0][j * 4 : j * 4 + 4]
                halo_ref[3 + j, c * ZD : (c + 1) * ZD, cols] = high[1][j * 4 : j * 4 + 4]


def insert(count, weights, geometry, phases, payload):
    vmem = pl.BlockSpec(memory_space=pltpu.VMEM)
    return pl.pallas_call(
        functools.partial(insert_kernel, count),
        out_shape=(
            jax.ShapeDtypeStruct((count, ZD, LINES, GRID), jnp.float32),
            jax.ShapeDtypeStruct((count, ZD, LINES, GRID), jnp.bfloat16),
            jax.ShapeDtypeStruct((count, ZD, LINES, GRID), jnp.bfloat16),
            jax.ShapeDtypeStruct((6, 8, GRID), jnp.float32),
        ),
        in_specs=[pl.BlockSpec(memory_space=pltpu.SMEM), vmem, vmem, vmem],
        out_specs=(vmem, vmem, vmem, vmem),
        scratch_shapes=[
            pltpu.VMEM((2, count * KC, GRID), jnp.bfloat16),
            pltpu.VMEM((2, count * MROWS, count * KC), jnp.bfloat16),
        ],
        compiler_params=pltpu.CompilerParams(vmem_limit_bytes=60 << 20),
        cost_estimate=pl.CostEstimate(
            flops=count * count * 4 * MROWS * KC * GRID, bytes_accessed=count * 5 << 20,
            transcendentals=0,
        ),
        name=f"insert{count}",
    )(weights, geometry, phases, payload)


def exchange_kernel(
    signs, mid_ref, up_ref, dn_ref, halo_ref, out_ref,
    from_low, from_high, halos, half, mirror, perm, back, send, recv,
):
    count = len(signs)
    kz, ky = lax.axis_index("kz"), lax.axis_index("ky")
    above, below = lax.rem(kz + 1, 16), lax.rem(kz + 15, 16)
    after, before = lax.rem(ky + 1, 16), lax.rem(ky + 15, 16)
    partner = {"kz": 15 - kz, "ky": 15 - ky}
    slabs = (below, kz, above)
    peers = [{"kz": above, "ky": ky}, {"kz": below, "ky": ky}]
    peers += [{"kz": s, "ky": r} for s in slabs for r in (before, after)]
    peers += [partner]
    barrier = pltpu.get_barrier_semaphore()
    for peer in peers:
        pl.semaphore_signal(barrier, inc=1, device_id=peer, device_id_type=MESH)
    pl.semaphore_wait(barrier, len(peers))

    def copy(source, target, number, peer):
        return pltpu.make_async_remote_copy(
            src_ref=source, dst_ref=target, send_sem=send.at[number], recv_sem=recv.at[number],
            device_id=peer, device_id_type=MESH,
        )

    edges = []
    for j in range(3):
        for side, target in ((0, before), (1, after)):
            number = side * 3 + j
            edges.append(
                copy(
                    halo_ref.at[number], halos.at[number], number,
                    {"kz": slabs[j], "ky": target},
                )
            )
    margins = [
        (
            copy(up_ref.at[c], from_low.at[c], 6 + 2 * c, peers[0]),
            copy(dn_ref.at[c], from_high.at[c], 7 + 2 * c, peers[1]),
        )
        for c in range(count)
    ]
    for item in edges + [item for pair in margins for item in pair]:
        item.start()

    @pl.loop(0, GRID // 128)
    def _(tile):
        rows = pl.multiple_of(tile * 128, 128)
        k = lax.broadcasted_iota(jnp.int32, (128, GRID), 0) + rows
        x = lax.broadcasted_iota(jnp.int32, (128, GRID), 1)
        wanted = jnp.where(k < SLICE, 2 * k, 2 * (k - SLICE) + 1)
        perm[pl.ds(rows, 128), :] = (x == wanted).astype(jnp.float32).astype(jnp.bfloat16)
        back[pl.ds(rows, 128), :] = (GRID - 1 - x == wanted).astype(jnp.float32).astype(jnp.bfloat16)

    for item in edges:
        item.wait()

    lower = jnp.where(kz > 0, 1.0, 0.0)
    upper = jnp.where(kz < 15, 1.0, 0.0)
    lines = lax.broadcasted_iota(jnp.int32, (LINES, 1), 0)
    copies = []
    for c in range(count):
        for item in margins[c]:
            item.wait()

        @pl.loop(0, ZD)
        def _(p):
            row = pl.ds(c * ZD + p, 1)
            total = mid_ref[c, p] + lower * from_low[c, p].astype(jnp.float32)
            total = total + upper * from_high[c, p].astype(jnp.float32)
            last = upper * halos[0, row, :] + halos[1, row, :] + lower * halos[2, row, :]
            start = upper * halos[3, row, :] + halos[4, row, :] + lower * halos[5, row, :]
            total = total + jnp.where(lines == LINES - 1, last, 0.0)
            total = total + jnp.where(lines == 0, start, 0.0)
            half[c, pl.ds(pl.multiple_of(p * LINES, LINES), LINES), :] = total.astype(jnp.bfloat16)

        item = copy(half.at[c], mirror.at[c], 6 + 2 * count + c, partner)
        item.start()
        copies.append(item)

    for c in range(count):

        @pl.loop(0, GRID // 256)
        def _(tile):
            cols = pl.ds(pl.multiple_of(tile * 256, 256), 256)
            out_ref[c, :, cols] = jnp.dot(
                half[c], perm[:, cols], preferred_element_type=jnp.float32
            )

    i = lax.broadcasted_iota(jnp.int32, (256, 256), 0)
    j = lax.broadcasted_iota(jnp.int32, (256, 256), 1)
    flip = (i + j == 255).astype(jnp.float32).astype(jnp.bfloat16)
    for c, sign in enumerate(signs):
        copies[c].wait()
        turned = jnp.dot(flip, mirror[c], preferred_element_type=jnp.float32)
        mirror[c] = turned.astype(jnp.bfloat16)

        @pl.loop(0, GRID // 256)
        def _(tile):
            cols = pl.ds(pl.multiple_of(tile * 256, 256), 256)
            out_ref[c, :, cols] += sign * jnp.dot(
                mirror[c], back[:, cols], preferred_element_type=jnp.float32
            )


def exchange(signs, mid, up, dn, halo):
    count = len(signs)
    vmem = pl.BlockSpec(memory_space=pltpu.VMEM)
    return pl.pallas_call(
        functools.partial(exchange_kernel, signs),
        out_shape=jax.ShapeDtypeStruct((count, ZD * LINES, GRID), jnp.float32),
        in_specs=[vmem] * 4,
        out_specs=vmem,
        scratch_shapes=[
            pltpu.VMEM((count, ZD, LINES, GRID), jnp.bfloat16),
            pltpu.VMEM((count, ZD, LINES, GRID), jnp.bfloat16),
            pltpu.VMEM((6, 8, GRID), jnp.float32),
            pltpu.VMEM((count, ZD * LINES, GRID), jnp.bfloat16),
            pltpu.VMEM((count, ZD * LINES, GRID), jnp.bfloat16),
            pltpu.VMEM((GRID, GRID), jnp.bfloat16),
            pltpu.VMEM((GRID, GRID), jnp.bfloat16),
            pltpu.SemaphoreType.DMA((6 + 3 * count,)),
            pltpu.SemaphoreType.DMA((6 + 3 * count,)),
        ],
        compiler_params=pltpu.CompilerParams(
            collective_id=count, has_side_effects=True, vmem_limit_bytes=60 << 20
        ),
        cost_estimate=pl.CostEstimate(
            flops=count * 4 * 256 * GRID * GRID, bytes_accessed=count * 20 << 20, transcendentals=0
        ),
        name=f"exchange{count}",
    )(mid, up, dn, halo)


def padded(
    slice_re, slice_im, slice_ctf, slice_dest, slice_plane, helix_index, slice_tilt, slice_shift
):
    slab_index = lax.axis_index("kz")
    held_count = slice_re.shape[0]
    ctf = slice_ctf.astype(jnp.float32)
    square = (ctf * ctf).astype(jnp.bfloat16)[:, None]
    pair = jnp.stack(
        [ctf * slice_re.astype(jnp.float32), ctf * slice_im.astype(jnp.float32)], axis=1
    ).astype(jnp.bfloat16)
    ones = jnp.ones((held_count,), jnp.float32)
    zeros = jnp.zeros((held_count,), jnp.float32)
    geometry = jnp.stack(
        [
            slice_plane.astype(jnp.float32),
            helix_index.astype(jnp.float32),
            ones,
            slice_tilt.astype(jnp.float32),
            slice_shift[0].astype(jnp.float32),
            slice_shift[1].astype(jnp.float32),
            zeros,
            zeros,
        ],
        axis=1,
    ).astype(jnp.bfloat16)
    target = slice_dest[:, 0]
    onehot = (target[:, None] == jnp.arange(SLABS)[None, :]).astype(jnp.int32)
    ranking = jnp.sum((jnp.cumsum(onehot, axis=0) - 1) * onehot, axis=1)
    position = target * CAP + ranking
    matches = (jnp.arange(SLOTS)[:, None] == position[None, :]).astype(jnp.int32)
    occupied = jnp.sum(matches, axis=1) > 0
    source_row = jnp.sum(matches * jnp.arange(held_count)[None, :], axis=1)

    def dispatch(values):
        picked = jnp.take(values, source_row, axis=0, mode="clip")
        return lax.all_to_all(picked, "kz", split_axis=0, concat_axis=0, tiled=True)

    slots = jnp.where(occupied[:, None], jnp.take(geometry, source_row, axis=0, mode="clip"), 0)
    arrived = lax.all_to_all(slots, "kz", split_axis=0, concat_axis=0, tiled=True)
    square = dispatch(square)
    pair = dispatch(pair)
    arrived = arrived.astype(jnp.float32)
    offset = arrived[:, 5:6]
    weights = kaiser(jnp.array([[0.0, 2.0, 1.0, -1.0]]) - offset)
    weights = weights.astype(jnp.bfloat16).astype(jnp.float32)
    band = slab_index * ZD + jnp.arange(16) - MZ
    angle = twist_step * (arrived[:, 1].astype(jnp.int32)[None, :] * band[:, None]).astype(
        jnp.float32
    )
    phases = jnp.repeat(jnp.concatenate([jnp.cos(angle), jnp.sin(angle)], axis=0), HALF, axis=1)
    spread = jnp.repeat(arrived.T, HALF, axis=1)
    weight = exchange((1.0,), *insert(1, weights, spread, phases, square))
    signal = exchange((1.0, -1.0), *insert(2, weights, spread, phases, pair))
    return jnp.concatenate([signal, weight], axis=0)


PLANE, HELIX, VALID, TILT, SHIFT_Y, SHIFT_X, DEST, TAPS, EXTRA = 0, 1, 2, 3, 4, 5, 6, 8, 12


def plan_kernel(dest, plane, helix, tilt, shift, table, rows, seen):
    lane = lax.broadcasted_iota(jnp.int32, (1, 128), 1)
    table[...] = jnp.zeros_like(table)
    for d in range(SLABS):
        seen[d] = 0
        rows[d] = 0
        rows[SLABS + d] = 0
    extra = jnp.int32(0)
    for i in range(SLABS):
        d = dest[i, 0]
        fields = (
            (PLANE, plane[i].astype(jnp.float32)), (HELIX, helix[i].astype(jnp.float32)),
            (VALID, 1.0), (TILT, tilt[i]), (SHIFT_Y, shift[0, i]), (SHIFT_X, shift[1, i]),
            (DEST, d.astype(jnp.float32)),
        )
        row = jnp.zeros((1, 128), jnp.float32)
        for index, value in fields:
            row = jnp.where(lane == index, value, row)
        before = seen[d]

        @pl.when(before == 0)
        def _():
            table[d, 0:1, :] = row
            rows[d] = i

        @pl.when((before > 0) & (extra < SPARE))
        def _():
            rows[SLABS + extra] = i
            for other in range(SLABS):
                table[other, pl.ds(1 + extra, 1), :] = row

        seen[d] = before + 1
        extra = extra + jnp.where(before > 0, 1, 0)
    lags = jnp.where(lane == TAPS + 1, 2.0, jnp.where(lane == TAPS + 2, 1.0, 0.0))
    lags = jnp.where(lane == TAPS + 3, -1.0, lags)
    for d in range(SLABS):
        block = table[d]
        taps = kaiser(lags - block[:, SHIFT_X : SHIFT_X + 1])
        taps = taps.astype(jnp.bfloat16).astype(jnp.float32)
        block = jnp.where((lane >= TAPS) & (lane < TAPS + 4), taps, block)
        table[d] = jnp.where(lane == EXTRA, extra.astype(jnp.float32), block)


def plan(dest, plane, helix, tilt, shift):
    smem = pl.BlockSpec(memory_space=pltpu.SMEM)
    return pl.pallas_call(
        plan_kernel,
        out_shape=(
            jax.ShapeDtypeStruct((SLABS, 8, 128), jnp.float32),
            jax.ShapeDtypeStruct((2 * SLABS,), jnp.int32),
        ),
        in_specs=[smem] * 5,
        out_specs=(pl.BlockSpec(memory_space=pltpu.VMEM), smem),
        scratch_shapes=[pltpu.SMEM((SLABS,), jnp.int32)],
        name="plan",
    )(dest, plane, helix, tilt.astype(jnp.float32), shift.astype(jnp.float32))


def dispatch_kernel(
    rows, table, re_ref, im_ref, ctf_ref, cap, spare, tables, outbox,
    send, recv, cap_send, cap_recv, tab_send, tab_recv,
):
    me = lax.axis_index("kz")
    side, core = me // 8, lax.rem(me, 2)
    column = lax.rem(me, 8) // 2

    def at(other_side, x, c):
        return other_side * 8 + lax.rem(x + 4, 4) * 2 + c

    across, twin = at(1 - side, column, core), at(side, column, 1 - core)
    right, left = at(side, column + 1, core), at(side, column - 1, core)
    far = at(side, column + 2, core)
    right_across, left_across = at(1 - side, column + 1, core), at(1 - side, column - 1, core)
    far_across = at(1 - side, column + 2, core)
    barrier = pltpu.get_barrier_semaphore()
    for r in range(1, SLABS):
        pl.semaphore_signal(
            barrier, inc=1, device_id={"kz": lax.rem(me + r, SLABS)}, device_id_type=MESH
        )

    def pack(row, target, place):
        ctf = ctf_ref[row].astype(jnp.float32)
        target[place, 0] = (ctf * re_ref[row].astype(jnp.float32)).astype(jnp.bfloat16)
        target[place, 1] = (ctf * im_ref[row].astype(jnp.float32)).astype(jnp.bfloat16)
        target[place, 2] = (ctf * ctf).astype(jnp.bfloat16)

    for j in range(SPARE):
        pack(rows[SLABS + j], spare, me * SPARE + j)
    pl.semaphore_wait(barrier, SLABS - 1)

    def pass_on(number, origin, target, part=(0, SPARE)):
        block = spare.at[pl.ds(origin * SPARE + part[0], part[1] - part[0])]
        item = pltpu.make_async_remote_copy(
            src_ref=block, dst_ref=block, send_sem=send.at[number], recv_sem=recv.at[number],
            device_id={"kz": target}, device_id_type=MESH,
        )
        item.start()
        return item

    lower, upper = (0, SPARE // 2), (SPARE // 2, SPARE)
    sent = {}
    sent[0] = pass_on(0, me, across)
    sent[1] = pass_on(1, me, right)
    sent[2] = pass_on(2, me, left)
    sent[3] = pass_on(3, me, twin)
    copies = []
    for r in range(1, SLABS):
        d = lax.rem(me + r, SLABS)
        item = pltpu.make_async_remote_copy(
            src_ref=table.at[d], dst_ref=tables.at[me], send_sem=tab_send.at[r],
            recv_sem=tab_recv.at[r], device_id={"kz": d}, device_id_type=MESH,
        )
        item.start()
        copies.append(item)
        pack(rows[d], outbox, d)
        item = pltpu.make_async_remote_copy(
            src_ref=outbox.at[d], dst_ref=cap.at[me], send_sem=cap_send.at[r],
            recv_sem=cap_recv.at[r], device_id={"kz": d}, device_id_type=MESH,
        )
        item.start()
        copies.append(item)
    pack(rows[me], cap, me)
    tables[me] = table[me]

    sent[0].wait_recv()
    sent[4] = pass_on(4, across, right)
    sent[5] = pass_on(5, across, left)
    sent[6] = pass_on(6, across, twin)
    sent[1].wait_recv()
    sent[7] = pass_on(7, left, right, lower)
    sent[8] = pass_on(8, left, twin)
    sent[2].wait_recv()
    sent[9] = pass_on(9, right, left, upper)
    sent[10] = pass_on(10, right, twin)
    sent[4].wait_recv()
    sent[11] = pass_on(11, left_across, right, lower)
    sent[12] = pass_on(12, left_across, twin)
    sent[5].wait_recv()
    sent[13] = pass_on(13, right_across, left, upper)
    sent[14] = pass_on(14, right_across, twin)
    sent[7].wait_recv()
    sent[15] = pass_on(15, far, twin, lower)
    sent[9].wait_recv()
    sent[16] = pass_on(16, far, twin, upper)
    sent[11].wait_recv()
    sent[17] = pass_on(17, far_across, twin, lower)
    sent[13].wait_recv()
    sent[18] = pass_on(18, far_across, twin, upper)
    for number in (3, 6, 8, 10, 12, 14, 15, 16, 17, 18):
        sent[number].wait_recv()
    for number in range(19):
        sent[number].wait_send()
    for item in copies:
        item.wait()


def dispatch_all(rows, table, slice_re, slice_im, slice_ctf):
    vmem = pl.BlockSpec(memory_space=pltpu.VMEM)
    dma = pltpu.SemaphoreType.DMA
    return pl.pallas_call(
        dispatch_kernel,
        out_shape=(
            jax.ShapeDtypeStruct((SLABS, 3, STRIP, SLICE), jnp.bfloat16),
            jax.ShapeDtypeStruct((SLABS * SPARE, 3, STRIP, SLICE), jnp.bfloat16),
            jax.ShapeDtypeStruct((SLABS, 8, 128), jnp.float32),
        ),
        in_specs=[pl.BlockSpec(memory_space=pltpu.SMEM)] + [vmem] * 4,
        out_specs=(vmem,) * 3,
        scratch_shapes=[pltpu.VMEM((SLABS, 3, STRIP, SLICE), jnp.bfloat16)]
        + [dma((19,)), dma((19,))] + [dma((SLABS,))] * 4,
        compiler_params=pltpu.CompilerParams(
            collective_id=4, has_side_effects=True, vmem_limit_bytes=40 << 20
        ),
        name="dispatch",
    )(rows, table, slice_re, slice_im, slice_ctf)


def fused_kernel(
    table, trig, cap, spare, out_ref,
    b, a, mid, up, dn, edge, from_low, from_high, halos, half, mirror, perm, back, send, recv,
):
    kz, ky = lax.axis_index("kz"), lax.axis_index("ky")
    above, below = lax.rem(kz + 1, 16), lax.rem(kz + 15, 16)
    after, before = lax.rem(ky + 1, 16), lax.rem(ky + 15, 16)
    partner = {"kz": 15 - kz, "ky": 15 - ky}
    slabs = (below, kz, above)
    peers = [{"kz": above, "ky": ky}, {"kz": below, "ky": ky}]
    peers += [{"kz": s, "ky": r} for s in slabs for r in (before, after)]
    peers += [partner]
    barrier = pltpu.get_barrier_semaphore()
    for peer in peers:
        pl.semaphore_signal(barrier, inc=1, device_id=peer, device_id_type=MESH)

    def copy(source, target, number, peer):
        return pltpu.make_async_remote_copy(
            src_ref=source, dst_ref=target, send_sem=send.at[number], recv_sem=recv.at[number],
            device_id=peer, device_id_type=MESH,
        )

    k = lax.broadcasted_iota(jnp.int32, (1, KA), 1)
    slot, local = k // HALF, k % HALF
    other = slot - SLABS
    place = jnp.where(slot < SLABS, slot * 8, (other // SPARE) * 8 + 1 + other % SPARE)
    pick = (lax.broadcasted_iota(jnp.int32, (SLABS * 8, KA), 0) == place).astype(jnp.float32)
    spread = lax.dot_general(
        table[...].astype(jnp.bfloat16), pick.astype(jnp.bfloat16), (((0,), (0,)), ((), ())),
        preferred_element_type=jnp.float32,
    )

    def field(index):
        return spread[index : index + 1]

    plane, tilt, shift, helix = field(PLANE), field(TILT), field(SHIFT_Y), field(HELIX)
    live = jnp.where(field(DEST) == kz.astype(jnp.float32), field(VALID), 0.0)
    level = (lax.broadcasted_iota(jnp.int32, (16, 1), 0) - MZ).astype(jnp.float32)
    line = lax.broadcasted_iota(jnp.int32, (32, 1), 0)
    main_y = kaiser((line - 2 * local).astype(jnp.float32) - shift)
    low_y = kaiser((-1 - 2 * local).astype(jnp.float32) - shift)
    high_y = kaiser((32 - 2 * local).astype(jnp.float32) - shift)
    cosine = jnp.zeros((16, KA), jnp.float32)
    sine = jnp.zeros((16, KA), jnp.float32)
    for h in range(8):
        cosine = jnp.where(helix == float(h), trig[:, h : h + 1], cosine)
        sine = jnp.where(helix == float(h), trig[:, 8 + h : 9 + h], sine)

    def along_z(q):
        row = ky * STRIP + q * HALF + local - SLICE // 2
        centre = plane + tilt * row.astype(jnp.float32) / (SLICE // 2)
        return kaiser(level - centre) * live

    blocks = [(MAIN, slice(0, 16), low_y), (MAIN + 16, slice(0, 16), high_y)]
    blocks += [(z * 32, slice(z, z + 1), main_y) for z in range(ZE)]

    def spread_slot(source, n, tab_row, first, channels):
        taps = table[pl.ds(tab_row, 1), :]
        wa, wb = taps[:, TAPS : TAPS + 1], taps[:, TAPS + 1 : TAPS + 2]
        wc, wd = taps[:, TAPS + 2 : TAPS + 3], taps[:, TAPS + 3 : TAPS + 4]
        for index, c in enumerate(channels):
            d = source[n, c].astype(jnp.float32)
            even = (wa * d + wb * pltpu.roll(d, 1, 1)).astype(jnp.bfloat16)
            odd = (wc * d + wd * pltpu.roll(d, SLICE - 1, 1)).astype(jnp.bfloat16)
            rows = pl.ds(pl.multiple_of(index * KA + first, HALF), HALF)
            for q in range(2):
                b[q, rows, 0:SLICE] = even[q * HALF : (q + 1) * HALF]
                b[q, rows, SLICE:GRID] = odd[q * HALF : (q + 1) * HALF]

    def spread_all(channels):
        @pl.loop(0, SLABS)
        def _(n):
            spread_slot(cap, n, n * 8, n * HALF, channels)

        @pl.loop(0, SLABS)
        def _(n):
            for j in range(SPARE):
                m = n * SPARE + j
                spread_slot(spare, m, n * 8 + 1 + j, (SLABS + m) * HALF, channels)

    lines = lax.broadcasted_iota(jnp.int32, (1, 32, 1), 1)

    def multiply(c, rows, depth):
        @pl.loop(0, GRID // 256)
        def _(tile):
            cols = pl.ds(pl.multiple_of(tile * 256, 256), 256)
            parts = [
                jnp.dot(a[q, rows, 0:depth], b[q, 0:depth, cols], preferred_element_type=jnp.float32)
                for q in range(2)
            ]
            low = [part[MAIN : MAIN + ZE] for part in parts]
            high = [part[MAIN + 16 : MAIN + 16 + ZE] for part in parts]
            main = [part[:MAIN].reshape(ZE, 32, 256) for part in parts]
            main[0] = main[0] + jnp.where(lines == 31, low[1][:, None, :], 0.0)
            main[1] = main[1] + jnp.where(lines == 0, high[0][:, None, :], 0.0)
            for q in range(2):
                span = slice(q * 32, q * 32 + 32)
                dn[c, :, span, cols] = main[q][0:MZ].astype(jnp.bfloat16)
                mid[c, :, span, cols] = main[q][MZ : MZ + ZD]
                up[c, :, span, cols] = main[q][MZ + ZD :].astype(jnp.bfloat16)
            for j in range(3):
                edge[c, j, 0:ZD, cols] = low[0][j * 4 : j * 4 + 4]
                edge[c, 3 + j, 0:ZD, cols] = high[1][j * 4 : j * 4 + 4]

    def send_margins(c):
        items = [
            copy(up.at[c], from_low.at[c], 9 * c, peers[0]),
            copy(dn.at[c], from_high.at[c], 9 * c + 1, peers[1]),
        ]
        for j in range(3):
            for side, target in ((0, before), (1, after)):
                index = side * 3 + j
                items.append(
                    copy(
                        edge.at[c, index], halos.at[c, index], 9 * c + 2 + index,
                        {"kz": slabs[j], "ky": target},
                    )
                )
        for item in items:
            item.start()
        return items

    lower = jnp.where(kz > 0, 1.0, 0.0)
    upper = jnp.where(kz < 15, 1.0, 0.0)
    last_line = lax.broadcasted_iota(jnp.int32, (LINES, 1), 0)

    def finish(c, items):
        for item in items:
            item.wait()

        @pl.loop(0, ZD)
        def _(p):
            row = pl.ds(p, 1)
            total = mid[c, p] + lower * from_low[c, p].astype(jnp.float32)
            total = total + upper * from_high[c, p].astype(jnp.float32)
            last = upper * halos[c, 0, row, :] + halos[c, 1, row, :] + lower * halos[c, 2, row, :]
            start = upper * halos[c, 3, row, :] + halos[c, 4, row, :] + lower * halos[c, 5, row, :]
            total = total + jnp.where(last_line == LINES - 1, last, 0.0)
            total = total + jnp.where(last_line == 0, start, 0.0)
            half[c, pl.ds(pl.multiple_of(p * LINES, LINES), LINES), :] = total.astype(jnp.bfloat16)

        item = copy(half.at[c], mirror.at[c], 9 * c + 8, partner)
        item.start()
        return item

    spread_all((2,))
    for q in range(2):
        along = along_z(q)
        for first, levels, value_y in blocks:
            size = 16 if first >= MAIN else 32
            a[q, first : first + size, 0:KA] = (along[levels] * value_y).astype(jnp.bfloat16)
    multiply(2, slice(0, MROWS), KA)
    pl.semaphore_wait(barrier, len(peers))
    weight_items = send_margins(2)

    spread_all((0, 1))
    for q in range(2):
        along = along_z(q)
        real, imag = along * cosine, along * sine
        for first, levels, value_y in blocks:
            size = 16 if first >= MAIN else 32
            rows = slice(first, first + size)
            again = slice(MROWS + first, MROWS + first + size)
            kr = (real[levels] * value_y).astype(jnp.bfloat16)
            ki = imag[levels] * value_y
            a[q, rows, 0:KA] = kr
            a[q, rows, KA : 2 * KA] = (-ki).astype(jnp.bfloat16)
            a[q, again, 0:KA] = ki.astype(jnp.bfloat16)
            a[q, again, KA : 2 * KA] = kr
    copies = {2: finish(2, weight_items)}
    multiply(0, slice(0, MROWS), 2 * KA)
    real_items = send_margins(0)
    multiply(1, slice(MROWS, 2 * MROWS), 2 * KA)
    imag_items = send_margins(1)

    @pl.loop(0, GRID // 128)
    def _(tile):
        rows = pl.multiple_of(tile * 128, 128)
        k = lax.broadcasted_iota(jnp.int32, (128, GRID), 0) + rows
        x = lax.broadcasted_iota(jnp.int32, (128, GRID), 1)
        wanted = jnp.where(k < SLICE, 2 * k, 2 * (k - SLICE) + 1)
        perm[pl.ds(rows, 128), :] = (x == wanted).astype(jnp.float32).astype(jnp.bfloat16)
        back[pl.ds(rows, 128), :] = (GRID - 1 - x == wanted).astype(jnp.float32).astype(jnp.bfloat16)

    copies[0] = finish(0, real_items)
    copies[1] = finish(1, imag_items)

    for c in range(3):

        @pl.loop(0, GRID // 256)
        def _(tile):
            cols = pl.ds(pl.multiple_of(tile * 256, 256), 256)
            out_ref[c, :, cols] = jnp.dot(
                half[c], perm[:, cols], preferred_element_type=jnp.float32
            )

    i = lax.broadcasted_iota(jnp.int32, (256, 256), 0)
    j = lax.broadcasted_iota(jnp.int32, (256, 256), 1)
    flip = (i + j == 255).astype(jnp.float32).astype(jnp.bfloat16)
    for c, sign in ((2, 1.0), (0, 1.0), (1, -1.0)):
        copies[c].wait()
        turned = jnp.dot(flip, mirror[c], preferred_element_type=jnp.float32)
        mirror[c] = turned.astype(jnp.bfloat16)

        @pl.loop(0, GRID // 256)
        def _(tile):
            cols = pl.ds(pl.multiple_of(tile * 256, 256), 256)
            out_ref[c, :, cols] += sign * jnp.dot(
                mirror[c], back[:, cols], preferred_element_type=jnp.float32
            )


def fused(table, trig, cap, spare):
    vmem = pl.BlockSpec(memory_space=pltpu.VMEM)
    slab = (3, ZD, LINES, GRID)
    flat = (3, ZD * LINES, GRID)
    return pl.pallas_call(
        fused_kernel,
        out_shape=jax.ShapeDtypeStruct(flat, jnp.float32),
        in_specs=[vmem] * 4,
        out_specs=vmem,
        scratch_shapes=[
            pltpu.VMEM((2, 2 * KA, GRID), jnp.bfloat16),
            pltpu.VMEM((2, 2 * MROWS, 2 * KA), jnp.bfloat16),
            pltpu.VMEM(slab, jnp.float32),
            pltpu.VMEM(slab, jnp.bfloat16),
            pltpu.VMEM(slab, jnp.bfloat16),
            pltpu.VMEM((3, 6, 8, GRID), jnp.float32),
            pltpu.VMEM(slab, jnp.bfloat16),
            pltpu.VMEM(slab, jnp.bfloat16),
            pltpu.VMEM((3, 6, 8, GRID), jnp.float32),
            pltpu.VMEM(flat, jnp.bfloat16),
            pltpu.VMEM(flat, jnp.bfloat16),
            pltpu.VMEM((GRID, GRID), jnp.bfloat16),
            pltpu.VMEM((GRID, GRID), jnp.bfloat16),
            pltpu.SemaphoreType.DMA((27,)),
            pltpu.SemaphoreType.DMA((27,)),
        ],
        compiler_params=pltpu.CompilerParams(
            collective_id=3, has_side_effects=True, vmem_limit_bytes=62 << 20
        ),
        name="fused",
    )(table, trig, cap, spare)


def balanced(slice_re, slice_im, slice_ctf, dest, plane, helix, tilt, shift):
    table, rows = plan(dest, plane, helix, tilt, shift)
    cap, spare, tables = dispatch_all(rows, table, slice_re, slice_im, slice_ctf)
    band = lax.axis_index("kz") * ZD + jnp.arange(16) - MZ
    angle = twist_step * (jnp.arange(8)[None, :] * band[:, None]).astype(jnp.float32)
    trig = jnp.concatenate([jnp.cos(angle), jnp.sin(angle)], axis=1)
    fits = jnp.max(tables[:, 0, EXTRA]) <= SPARE
    return tables.reshape(SLABS * 8, 128), trig, cap, spare, fits


def per_device(*arguments):
    table, trig, cap, spare, fits = balanced(*arguments)
    out = lax.cond(
        fits,
        lambda: fused(table, trig, cap, spare),
        lambda: padded(*arguments),
    )
    return out.reshape(3, ZD, LINES, GRID)


def solution(mesh):
    placed = (
        P("kz", "ky", None),
        P("kz", "ky", None),
        P("kz", "ky", None),
        P("kz", None),
        P("kz"),
        P("kz"),
        P("kz"),
        P(None, "kz"),
    )
    return jax.shard_map(
        per_device, mesh=mesh, in_specs=placed, out_specs=P(None, "kz", "ky", None), check_vma=False
    )
```

time: 261 us -> 182 us (0.70)
  waiting for transfers between devices: 81.2 us -> 0 us
  Pallas kernels: 137 us -> 171 us
  starting transfers between devices: 15.8 us -> 0 us
  other arithmetic: 13.5 us -> 3.25 us
  local copies, waits for them, and re-layouts: 12.4 us -> 6.81 us
    all_to_all x2 -> x0, waiting for transfers between devices: 81.2 us -> none  [the longest x1 81.2 us: per_device(): lax.all_to_all(jnp.take(data, source_row, axis=0), 'kz', split_axis=0, co...]
    pallas_call x2 -> x3, Pallas kernels: 137 us -> 171 us  [the longest x1 105 us: fused(): pl.pallas_call(fused_kernel, out_shape=jax.ShapeDtypeStruct(flat, jnp.flo...]
    all_to_all x2 -> x0, starting transfers between devices: 15.8 us -> none  [the longest x1 8.45 us: per_device(): lax.all_to_all(slots, 'kz', split_axis=0, concat_axis=0, tiled=True)]
    select_n x3 -> x0, other arithmetic: 6.82 us -> none  [the longest x1 6.11 us: per_device(): jnp.take(data, source_row, axis=0)]
    gather x2 -> x0, local copies, waits for them, and re-layouts: 4.24 us -> none  [the longest x1 3.61 us: per_device(): jnp.take(data, source_row, axis=0)]
    another operation x5 -> x0, other arithmetic: 3.29 us -> none  [the longest x2 1.93 us: per_device(): jnp.stack([ctf * slice_re.astype(jnp.float32), ctf * slice_im.astype(jnp....]
    unnamed x3 -> x6, local copies, waits for them, and re-layouts: 3.97 us -> 6.81 us
  transfers between devices with their start and end apart: 2 -> 0, of which waited for: 1 -> 0; matrix products, arithmetic and copies ran while one was open for 6% -> 0% of each run, Pallas kernels for 0% -> 0%
where the time goes in v2:
time: 182 us
  Pallas kernels  171 us (94%)
  local copies, waits for them, and re-layouts  6.81 us (4%)
  other arithmetic  3.25 us (2%)
    pallas_call x1, Pallas kernels, fused(): pl.pallas_call(fused_kernel, out_shape=jax.ShapeDtypeStruct(flat, jnp.flo...  105 us
    pallas_call x1, Pallas kernels, dispatch_all(): pl.pallas_call(dispatch_kernel, out_shape=(jax.ShapeDtypeStruct((SLABS, 3...  64 us
    unnamed x6, local copies, waits for them, and re-layouts  6.81 us

profile of v2, /device:TPU:1, one launch (start us, length us, event | category | flops | bytes accessed | tf_op | source)
XLA Modules:
  0.0 181.8 jit_solution(17600331599069153572)
XLA Ops:
  0.0 1.3 copy.58.dest
  1.3 1.2 convert_element_type.89.shift
  2.5 1.2 convert_element_type.88.tilt
  3.7 2.0 %plan.1 = (f32[16,8,128]{2,1,0:T(8,128)}, s32[32]{0:T(128)}) custom-call(s32[16,1]{1,0:T(8,128)} %copy.58.dest, s32[16]{0:T(128)} %plane.1, s32[16]{0:T(128)} %helix.1, f32[16]{0:T(128)} %convert_element_type.88.tilt, f32[2,16]{1,0:T(2,128)} %convert_element_type.89.shift), custom_call_target="tpu_custom_call" | custom-call | tf_op jit(solution)/shard_map/plan/pallas_call | solution.py:388
  5.7 0.0 copy-start
  5.7 0.8 copy-done
  6.5 0.0 copy-start.1
  6.5 0.7 copy-done.1
  7.2 64.0 %dispatch.1 = (bf16[16,3,32,512]{3,2,1,0:T(8,128)(2,1)}, bf16[64,3,32,512]{3,2,1,0:T(8,128)(2,1)}, f32[16,8,128]{2,1,0:T(8,128)S(1)}) custom-call(s32[32]{0:T(128)S(1)} %copy-done.1, f32[16,8,128]{2,1,0:T(8,128)S(1)} %copy-done, bf16[16,32,512]{2,1,0:T(8,128)(2,1)} %re_ref.1, bf16[16,32,512]{2,1,0:T(8,128)(2,1)} %im_ref.1, bf16[16,32,512]{2,1,0:T(8,128)(2,1)} %ctf_ref.1), custom_call_target="tpu_custom_call" | custom-call | tf_op jit(solution)/shard_map/dispatch/pallas_call | solution.py:502
  71.3 0.1 fusion.11
  71.4 0.1 pad_maximum_fusion.3
  71.5 0.7 slice_reduce_fusion.1
  72.8 105.0 %conditional.1 = (f32[3,4,64,1024]{3,2,1,0:T(8,128)}) conditional(s32[]{:T(128)} %convert_element_type.90, ((), s32[16,1]{0,1:T(1,128)}, s32[16]{0:T(128)}, s32[16]{0:T(128)}, bf16[16]{0:T(256)(128)(2,1)}, /*index=5*/bf16[2,16]{1,0:T(2,128)(2,1)}, bf16[16,32,512]{2,1,0:T(8,128)(2,1)}, bf16[16,32,512]{2,1,0:T(8,128)(2,1)}, ...), branch_computations={%region_1.6_spmd, %region_6.7_spmd} | conditional | flops 11949080576 | bytes 134823520 | solution.py:777
  73.1 104.8 %fused.1 = f32[3,256,1024]{2,1,0:T(8,128)} custom-call(f32[128,128]{1,0:T(8,128)S(1)} %bitcast.28, f32[16,16]{1,0:T(8,128)S(1)} %get-tuple-element.54.trig, bf16[16,3,32,512]{3,2,1,0:T(8,128)(2,1)} %get-tuple-element.55.cap, bf16[64,3,32,512]{3,2,1,0:T(8,128)(2,1)} %get-tuple-element.56.spare), custom_call_target="tpu_custom_call" | custom-call | tf_op jit(solution)/shard_map/cond/branch_1_fun/fused/pallas_call | solution.py:736
  177.8 4.0 %copy.62 = f32[3,4,64,1024]{3,2,1,0:T(8,128)} copy(f32[3,4,64,1024]{3,2,1,0:T(8,128)} %get-tuple-element.67) | data formatting | bytes 6291456
  (1 shorter events, 0.0 us)
Async XLA Ops:
  5.7 0.8 copy-start
  6.5 0.7 copy-start.1

commit v3 on v2

--- a/solution.py
+++ b/solution.py
@@ -149,10 +149,9 @@
 
 
 def exchange_kernel(
-    signs, mid_ref, up_ref, dn_ref, halo_ref, out_ref,
+    count, mid_ref, up_ref, dn_ref, halo_ref, own_ref, back_ref,
     from_low, from_high, halos, half, mirror, perm, back, send, recv,
 ):
-    count = len(signs)
     kz, ky = lax.axis_index("kz"), lax.axis_index("ky")
     above, below = lax.rem(kz + 1, 16), lax.rem(kz + 15, 16)
     after, before = lax.rem(ky + 1, 16), lax.rem(ky + 15, 16)
@@ -232,14 +231,13 @@
         @pl.loop(0, GRID // 256)
         def _(tile):
             cols = pl.ds(pl.multiple_of(tile * 256, 256), 256)
-            out_ref[c, :, cols] = jnp.dot(
-                half[c], perm[:, cols], preferred_element_type=jnp.float32
-            )
+            own = jnp.dot(half[c], perm[:, cols], preferred_element_type=jnp.float32)
+            own_ref[c, :, cols] = own.astype(jnp.bfloat16)
 
     i = lax.broadcasted_iota(jnp.int32, (256, 256), 0)
     j = lax.broadcasted_iota(jnp.int32, (256, 256), 1)
     flip = (i + j == 255).astype(jnp.float32).astype(jnp.bfloat16)
-    for c, sign in enumerate(signs):
+    for c in range(count):
         copies[c].wait()
         turned = jnp.dot(flip, mirror[c], preferred_element_type=jnp.float32)
         mirror[c] = turned.astype(jnp.bfloat16)
@@ -247,19 +245,18 @@
         @pl.loop(0, GRID // 256)
         def _(tile):
             cols = pl.ds(pl.multiple_of(tile * 256, 256), 256)
-            out_ref[c, :, cols] += sign * jnp.dot(
-                mirror[c], back[:, cols], preferred_element_type=jnp.float32
-            )
-
-
-def exchange(signs, mid, up, dn, halo):
-    count = len(signs)
+            other = jnp.dot(mirror[c], back[:, cols], preferred_element_type=jnp.float32)
+            back_ref[c, :, cols] = other.astype(jnp.bfloat16)
+
+
+def exchange(mid, up, dn, halo):
+    count = mid.shape[0]
     vmem = pl.BlockSpec(memory_space=pltpu.VMEM)
     return pl.pallas_call(
-        functools.partial(exchange_kernel, signs),
-        out_shape=jax.ShapeDtypeStruct((count, ZD * LINES, GRID), jnp.float32),
+        functools.partial(exchange_kernel, count),
+        out_shape=(jax.ShapeDtypeStruct((count, ZD * LINES, GRID), jnp.bfloat16),) * 2,
         in_specs=[vmem] * 4,
-        out_specs=vmem,
+        out_specs=(vmem,) * 2,
         scratch_shapes=[
             pltpu.VMEM((count, ZD, LINES, GRID), jnp.bfloat16),
             pltpu.VMEM((count, ZD, LINES, GRID), jnp.bfloat16),
@@ -332,15 +329,15 @@
     )
     phases = jnp.repeat(jnp.concatenate([jnp.cos(angle), jnp.sin(angle)], axis=0), HALF, axis=1)
     spread = jnp.repeat(arrived.T, HALF, axis=1)
-    weight = exchange((1.0,), *insert(1, weights, spread, phases, square))
-    signal = exchange((1.0, -1.0), *insert(2, weights, spread, phases, pair))
-    return jnp.concatenate([signal, weight], axis=0)
+    weight = exchange(*insert(1, weights, spread, phases, square))
+    signal = exchange(*insert(2, weights, spread, phases, pair))
+    return [jnp.concatenate(parts, axis=0) for parts in zip(signal, weight)]
 
 
 PLANE, HELIX, VALID, TILT, SHIFT_Y, SHIFT_X, DEST, TAPS, EXTRA = 0, 1, 2, 3, 4, 5, 6, 8, 12
 
 
-def plan_kernel(dest, plane, helix, tilt, shift, table, rows, seen):
+def plan_kernel(numbers, reals, table, rows, seen):
     lane = lax.broadcasted_iota(jnp.int32, (1, 128), 1)
     table[...] = jnp.zeros_like(table)
     for d in range(SLABS):
@@ -349,10 +346,11 @@
         rows[SLABS + d] = 0
     extra = jnp.int32(0)
     for i in range(SLABS):
-        d = dest[i, 0]
+        d = numbers[0, i]
         fields = (
-            (PLANE, plane[i].astype(jnp.float32)), (HELIX, helix[i].astype(jnp.float32)),
-            (VALID, 1.0), (TILT, tilt[i]), (SHIFT_Y, shift[0, i]), (SHIFT_X, shift[1, i]),
+            (PLANE, numbers[1, i].astype(jnp.float32)),
+            (HELIX, numbers[2, i].astype(jnp.float32)),
+            (VALID, 1.0), (TILT, reals[0, i]), (SHIFT_Y, reals[1, i]), (SHIFT_X, reals[2, i]),
             (DEST, d.astype(jnp.float32)),
         )
         row = jnp.zeros((1, 128), jnp.float32)
@@ -391,20 +389,24 @@
             jax.ShapeDtypeStruct((SLABS, 8, 128), jnp.float32),
             jax.ShapeDtypeStruct((2 * SLABS,), jnp.int32),
         ),
-        in_specs=[smem] * 5,
+        in_specs=[smem] * 2,
         out_specs=(pl.BlockSpec(memory_space=pltpu.VMEM), smem),
         scratch_shapes=[pltpu.SMEM((SLABS,), jnp.int32)],
         name="plan",
-    )(dest, plane, helix, tilt.astype(jnp.float32), shift.astype(jnp.float32))
-
-
-def dispatch_kernel(
-    rows, table, re_ref, im_ref, ctf_ref, cap, spare, tables, outbox,
-    send, recv, cap_send, cap_recv, tab_send, tab_recv,
+    )(
+        jnp.stack([dest[:, 0], plane, helix]),
+        jnp.concatenate([tilt[None], shift], axis=0).astype(jnp.float32),
+    )
+
+
+def whole_kernel(
+    rows, table, trig, re_ref, im_ref, ctf_ref, own_ref, back_ref, tables,
+    outbox, cap, spare, b, bw, a, aw, mid, up, dn, edge, from_low, from_high, halos, half, mirror,
+    perm, back, send, recv, hop_send, hop_recv, cap_send, cap_recv, tab_send, tab_recv,
 ):
-    me = lax.axis_index("kz")
-    side, core = me // 8, lax.rem(me, 2)
-    column = lax.rem(me, 8) // 2
+    kz, ky = lax.axis_index("kz"), lax.axis_index("ky")
+    side, core = kz // 8, lax.rem(kz, 2)
+    column = lax.rem(kz, 8) // 2
 
     def at(other_side, x, c):
         return other_side * 8 + lax.rem(x + 4, 4) * 2 + c
@@ -414,130 +416,120 @@
     far = at(side, column + 2, core)
     right_across, left_across = at(1 - side, column + 1, core), at(1 - side, column - 1, core)
     far_across = at(1 - side, column + 2, core)
-    barrier = pltpu.get_barrier_semaphore()
-    for r in range(1, SLABS):
-        pl.semaphore_signal(
-            barrier, inc=1, device_id={"kz": lax.rem(me + r, SLABS)}, device_id_type=MESH
-        )
-
-    def pack(row, target, place):
-        ctf = ctf_ref[row].astype(jnp.float32)
-        target[place, 0] = (ctf * re_ref[row].astype(jnp.float32)).astype(jnp.bfloat16)
-        target[place, 1] = (ctf * im_ref[row].astype(jnp.float32)).astype(jnp.bfloat16)
-        target[place, 2] = (ctf * ctf).astype(jnp.bfloat16)
-
-    for j in range(SPARE):
-        pack(rows[SLABS + j], spare, me * SPARE + j)
-    pl.semaphore_wait(barrier, SLABS - 1)
-
-    def pass_on(number, origin, target, part=(0, SPARE)):
-        block = spare.at[pl.ds(origin * SPARE + part[0], part[1] - part[0])]
-        item = pltpu.make_async_remote_copy(
-            src_ref=block, dst_ref=block, send_sem=send.at[number], recv_sem=recv.at[number],
-            device_id={"kz": target}, device_id_type=MESH,
-        )
-        item.start()
-        return item
-
-    lower, upper = (0, SPARE // 2), (SPARE // 2, SPARE)
-    sent = {}
-    sent[0] = pass_on(0, me, across)
-    sent[1] = pass_on(1, me, right)
-    sent[2] = pass_on(2, me, left)
-    sent[3] = pass_on(3, me, twin)
-    copies = []
-    for r in range(1, SLABS):
-        d = lax.rem(me + r, SLABS)
-        item = pltpu.make_async_remote_copy(
-            src_ref=table.at[d], dst_ref=tables.at[me], send_sem=tab_send.at[r],
-            recv_sem=tab_recv.at[r], device_id={"kz": d}, device_id_type=MESH,
-        )
-        item.start()
-        copies.append(item)
-        pack(rows[d], outbox, d)
-        item = pltpu.make_async_remote_copy(
-            src_ref=outbox.at[d], dst_ref=cap.at[me], send_sem=cap_send.at[r],
-            recv_sem=cap_recv.at[r], device_id={"kz": d}, device_id_type=MESH,
-        )
-        item.start()
-        copies.append(item)
-    pack(rows[me], cap, me)
-    tables[me] = table[me]
-
-    sent[0].wait_recv()
-    sent[4] = pass_on(4, across, right)
-    sent[5] = pass_on(5, across, left)
-    sent[6] = pass_on(6, across, twin)
-    sent[1].wait_recv()
-    sent[7] = pass_on(7, left, right, lower)
-    sent[8] = pass_on(8, left, twin)
-    sent[2].wait_recv()
-    sent[9] = pass_on(9, right, left, upper)
-    sent[10] = pass_on(10, right, twin)
-    sent[4].wait_recv()
-    sent[11] = pass_on(11, left_across, right, lower)
-    sent[12] = pass_on(12, left_across, twin)
-    sent[5].wait_recv()
-    sent[13] = pass_on(13, right_across, left, upper)
-    sent[14] = pass_on(14, right_across, twin)
-    sent[7].wait_recv()
-    sent[15] = pass_on(15, far, twin, lower)
-    sent[9].wait_recv()
-    sent[16] = pass_on(16, far, twin, upper)
-    sent[11].wait_recv()
-    sent[17] = pass_on(17, far_across, twin, lower)
-    sent[13].wait_recv()
-    sent[18] = pass_on(18, far_across, twin, upper)
-    for number in (3, 6, 8, 10, 12, 14, 15, 16, 17, 18):
-        sent[number].wait_recv()
-    for number in range(19):
-        sent[number].wait_send()
-    for item in copies:
-        item.wait()
-
-
-def dispatch_all(rows, table, slice_re, slice_im, slice_ctf):
-    vmem = pl.BlockSpec(memory_space=pltpu.VMEM)
-    dma = pltpu.SemaphoreType.DMA
-    return pl.pallas_call(
-        dispatch_kernel,
-        out_shape=(
-            jax.ShapeDtypeStruct((SLABS, 3, STRIP, SLICE), jnp.bfloat16),
-            jax.ShapeDtypeStruct((SLABS * SPARE, 3, STRIP, SLICE), jnp.bfloat16),
-            jax.ShapeDtypeStruct((SLABS, 8, 128), jnp.float32),
-        ),
-        in_specs=[pl.BlockSpec(memory_space=pltpu.SMEM)] + [vmem] * 4,
-        out_specs=(vmem,) * 3,
-        scratch_shapes=[pltpu.VMEM((SLABS, 3, STRIP, SLICE), jnp.bfloat16)]
-        + [dma((19,)), dma((19,))] + [dma((SLABS,))] * 4,
-        compiler_params=pltpu.CompilerParams(
-            collective_id=4, has_side_effects=True, vmem_limit_bytes=40 << 20
-        ),
-        name="dispatch",
-    )(rows, table, slice_re, slice_im, slice_ctf)
-
-
-def fused_kernel(
-    table, trig, cap, spare, out_ref,
-    b, a, mid, up, dn, edge, from_low, from_high, halos, half, mirror, perm, back, send, recv,
-):
-    kz, ky = lax.axis_index("kz"), lax.axis_index("ky")
+
     above, below = lax.rem(kz + 1, 16), lax.rem(kz + 15, 16)
     after, before = lax.rem(ky + 1, 16), lax.rem(ky + 15, 16)
     partner = {"kz": 15 - kz, "ky": 15 - ky}
     slabs = (below, kz, above)
-    peers = [{"kz": above, "ky": ky}, {"kz": below, "ky": ky}]
+    peers = [{"kz": lax.rem(kz + r, SLABS), "ky": ky} for r in range(1, SLABS)]
     peers += [{"kz": s, "ky": r} for s in slabs for r in (before, after)]
     peers += [partner]
     barrier = pltpu.get_barrier_semaphore()
     for peer in peers:
         pl.semaphore_signal(barrier, inc=1, device_id=peer, device_id_type=MESH)
 
-    def copy(source, target, number, peer):
-        return pltpu.make_async_remote_copy(
-            src_ref=source, dst_ref=target, send_sem=send.at[number], recv_sem=recv.at[number],
-            device_id=peer, device_id_type=MESH,
+    def pack_signal(row, target, place):
+        ctf = ctf_ref[row].astype(jnp.float32)
+        target[place, 0] = (ctf * re_ref[row].astype(jnp.float32)).astype(jnp.bfloat16)
+        target[place, 1] = (ctf * im_ref[row].astype(jnp.float32)).astype(jnp.bfloat16)
+
+    def pack_weight(row, target, place):
+        ctf = ctf_ref[row].astype(jnp.float32)
+        target[place, 2] = (ctf * ctf).astype(jnp.bfloat16)
+
+    for j in range(SPARE):
+        pack_weight(rows[SLABS + j], spare, kz * SPARE + j)
+    pl.semaphore_wait(barrier, len(peers))
+
+    channels = (slice(2, 3), slice(0, 2))
+    sent = {}
+
+    def pass_on(group, number, origin, target, part=(0, SPARE)):
+        block = spare.at[pl.ds(origin * SPARE + part[0], part[1] - part[0]), channels[group]]
+        item = pltpu.make_async_remote_copy(
+            src_ref=block, dst_ref=block, send_sem=hop_send.at[group, number],
+            recv_sem=hop_recv.at[group, number], device_id={"kz": target}, device_id_type=MESH,
         )
+        item.start()
+        sent[group, number] = item
+
+    def arrive(group, *numbers):
+        for number in numbers:
+            sent[group, number].wait_recv()
+
+    halves = ((0, SPARE // 2), (SPARE // 2, SPARE))
+
+    def hop_one(g):
+        pass_on(g, 0, kz, across)
+        pass_on(g, 1, kz, right)
+        pass_on(g, 2, kz, left)
+        pass_on(g, 3, kz, twin)
+
+    def hop_two(g):
+        arrive(g, 0)
+        pass_on(g, 4, across, right)
+        pass_on(g, 5, across, left)
+        pass_on(g, 6, across, twin)
+        arrive(g, 1)
+        pass_on(g, 7, left, right, halves[0])
+        pass_on(g, 8, left, twin)
+        arrive(g, 2)
+        pass_on(g, 9, right, left, halves[1])
+        pass_on(g, 10, right, twin)
+
+    def hop_three(g):
+        arrive(g, 4)
+        pass_on(g, 11, left_across, right, halves[0])
+        pass_on(g, 12, left_across, twin)
+        arrive(g, 5)
+        pass_on(g, 13, right_across, left, halves[1])
+        pass_on(g, 14, right_across, twin)
+        arrive(g, 7)
+        pass_on(g, 15, far, twin, halves[0])
+        arrive(g, 9)
+        pass_on(g, 16, far, twin, halves[1])
+
+    def hop_four(g):
+        arrive(g, 11)
+        pass_on(g, 17, far_across, twin, halves[0])
+        arrive(g, 13)
+        pass_on(g, 18, far_across, twin, halves[1])
+
+    direct = {0: [], 1: []}
+
+    def send_caps(g, pack):
+        for r in range(1, SLABS):
+            d = lax.rem(kz + r, SLABS)
+            pack(rows[d], outbox, d)
+            item = pltpu.make_async_remote_copy(
+                src_ref=outbox.at[d, channels[g]], dst_ref=cap.at[kz, channels[g]],
+                send_sem=cap_send.at[g, r], recv_sem=cap_recv.at[g, r],
+                device_id={"kz": d}, device_id_type=MESH,
+            )
+            item.start()
+            direct[g].append(item)
+        pack(rows[kz], cap, kz)
+
+    hop_one(0)
+    labels = []
+    for r in range(1, SLABS):
+        d = lax.rem(kz + r, SLABS)
+        item = pltpu.make_async_remote_copy(
+            src_ref=table.at[d], dst_ref=tables.at[kz], send_sem=tab_send.at[r],
+            recv_sem=tab_recv.at[r], device_id={"kz": d}, device_id_type=MESH,
+        )
+        item.start()
+        labels.append(item)
+    tables[kz] = table[kz]
+    send_caps(0, pack_weight)
+    for j in range(SPARE):
+        pack_signal(rows[SLABS + j], spare, kz * SPARE + j)
+    hop_two(0)
+    hop_one(1)
+    send_caps(1, pack_signal)
+    hop_three(0)
+    for item in labels:
+        item.wait()
 
     k = lax.broadcasted_iota(jnp.int32, (1, KA), 1)
     slot, local = k // HALF, k % HALF
@@ -545,8 +537,8 @@
     place = jnp.where(slot < SLABS, slot * 8, (other // SPARE) * 8 + 1 + other % SPARE)
     pick = (lax.broadcasted_iota(jnp.int32, (SLABS * 8, KA), 0) == place).astype(jnp.float32)
     spread = lax.dot_general(
-        table[...].astype(jnp.bfloat16), pick.astype(jnp.bfloat16), (((0,), (0,)), ((), ())),
-        preferred_element_type=jnp.float32,
+        tables[...].reshape(SLABS * 8, 128).astype(jnp.bfloat16), pick.astype(jnp.bfloat16),
+        (((0,), (0,)), ((), ())), preferred_element_type=jnp.float32,
     )
 
     def field(index):
@@ -573,38 +565,47 @@
     blocks = [(MAIN, slice(0, 16), low_y), (MAIN + 16, slice(0, 16), high_y)]
     blocks += [(z * 32, slice(z, z + 1), main_y) for z in range(ZE)]
 
-    def spread_slot(source, n, tab_row, first, channels):
-        taps = table[pl.ds(tab_row, 1), :]
+    def spread_slot(source, n, owner, index, first, group):
+        taps = tables[owner, pl.ds(index, 1), :]
         wa, wb = taps[:, TAPS : TAPS + 1], taps[:, TAPS + 1 : TAPS + 2]
         wc, wd = taps[:, TAPS + 2 : TAPS + 3], taps[:, TAPS + 3 : TAPS + 4]
-        for index, c in enumerate(channels):
+        for number, c in enumerate((2,) if group == 0 else (0, 1)):
             d = source[n, c].astype(jnp.float32)
             even = (wa * d + wb * pltpu.roll(d, 1, 1)).astype(jnp.bfloat16)
             odd = (wc * d + wd * pltpu.roll(d, SLICE - 1, 1)).astype(jnp.bfloat16)
-            rows = pl.ds(pl.multiple_of(index * KA + first, HALF), HALF)
+            rows = pl.ds(pl.multiple_of(number * KA + first, HALF), HALF)
+            target = bw if group == 0 else b
             for q in range(2):
-                b[q, rows, 0:SLICE] = even[q * HALF : (q + 1) * HALF]
-                b[q, rows, SLICE:GRID] = odd[q * HALF : (q + 1) * HALF]
-
-    def spread_all(channels):
+                target[q, rows, 0:SLICE] = even[q * HALF : (q + 1) * HALF]
+                target[q, rows, SLICE:GRID] = odd[q * HALF : (q + 1) * HALF]
+
+    def spread_caps(group):
+        for item in direct[group]:
+            item.wait()
+
         @pl.loop(0, SLABS)
         def _(n):
-            spread_slot(cap, n, n * 8, n * HALF, channels)
-
-        @pl.loop(0, SLABS)
-        def _(n):
+            spread_slot(cap, n, n, 0, n * HALF, group)
+
+    def spread_line(group, line_core):
+        @pl.loop(0, SLABS // 2)
+        def _(i):
+            owner = 2 * i + line_core
             for j in range(SPARE):
-                m = n * SPARE + j
-                spread_slot(spare, m, n * 8 + 1 + j, (SLABS + m) * HALF, channels)
+                m = owner * SPARE + j
+                spread_slot(spare, m, owner, 1 + j, (SLABS + m) * HALF, group)
 
     lines = lax.broadcasted_iota(jnp.int32, (1, 32, 1), 1)
 
-    def multiply(c, rows, depth):
+    def multiply(c, left_side, right_side, rows):
         @pl.loop(0, GRID // 256)
         def _(tile):
             cols = pl.ds(pl.multiple_of(tile * 256, 256), 256)
             parts = [
-                jnp.dot(a[q, rows, 0:depth], b[q, 0:depth, cols], preferred_element_type=jnp.float32)
+                jnp.dot(
+                    left_side[q, rows, :], right_side[q, :, cols],
+                    preferred_element_type=jnp.float32,
+                )
                 for q in range(2)
             ]
             low = [part[MAIN : MAIN + ZE] for part in parts]
@@ -621,14 +622,20 @@
                 edge[c, j, 0:ZD, cols] = low[0][j * 4 : j * 4 + 4]
                 edge[c, 3 + j, 0:ZD, cols] = high[1][j * 4 : j * 4 + 4]
 
+    def copy(source, target, number, peer):
+        return pltpu.make_async_remote_copy(
+            src_ref=source, dst_ref=target, send_sem=send.at[number], recv_sem=recv.at[number],
+            device_id=peer, device_id_type=MESH,
+        )
+
     def send_margins(c):
         items = [
-            copy(up.at[c], from_low.at[c], 9 * c, peers[0]),
-            copy(dn.at[c], from_high.at[c], 9 * c + 1, peers[1]),
+            copy(up.at[c], from_low.at[c], 9 * c, {"kz": above, "ky": ky}),
+            copy(dn.at[c], from_high.at[c], 9 * c + 1, {"kz": below, "ky": ky}),
         ]
         for j in range(3):
-            for side, target in ((0, before), (1, after)):
-                index = side * 3 + j
+            for end, target in ((0, before), (1, after)):
+                index = end * 3 + j
                 items.append(
                     copy(
                         edge.at[c, index], halos.at[c, index], 9 * c + 2 + index,
@@ -662,35 +669,45 @@
         item.start()
         return item
 
-    spread_all((2,))
     for q in range(2):
         along = along_z(q)
         for first, levels, value_y in blocks:
             size = 16 if first >= MAIN else 32
-            a[q, first : first + size, 0:KA] = (along[levels] * value_y).astype(jnp.bfloat16)
-    multiply(2, slice(0, MROWS), KA)
-    pl.semaphore_wait(barrier, len(peers))
+            aw[q, first : first + size, :] = (along[levels] * value_y).astype(jnp.bfloat16)
+    hop_four(0)
+    hop_two(1)
+    spread_caps(0)
+    spread_line(0, core)
+    arrive(0, 3, 6, 8, 10, 12, 14, 15, 16, 17, 18)
+    spread_line(0, 1 - core)
+    hop_three(1)
+    multiply(2, aw, bw, slice(0, MROWS))
     weight_items = send_margins(2)
-
-    spread_all((0, 1))
+    hop_four(1)
+    spread_caps(1)
     for q in range(2):
         along = along_z(q)
         real, imag = along * cosine, along * sine
         for first, levels, value_y in blocks:
             size = 16 if first >= MAIN else 32
-            rows = slice(first, first + size)
-            again = slice(MROWS + first, MROWS + first + size)
+            rows_re = slice(first, first + size)
+            rows_im = slice(MROWS + first, MROWS + first + size)
             kr = (real[levels] * value_y).astype(jnp.bfloat16)
             ki = imag[levels] * value_y
-            a[q, rows, 0:KA] = kr
-            a[q, rows, KA : 2 * KA] = (-ki).astype(jnp.bfloat16)
-            a[q, again, 0:KA] = ki.astype(jnp.bfloat16)
-            a[q, again, KA : 2 * KA] = kr
+            a[q, rows_re, 0:KA] = kr
+            a[q, rows_re, KA : 2 * KA] = (-ki).astype(jnp.bfloat16)
+            a[q, rows_im, 0:KA] = ki.astype(jnp.bfloat16)
+            a[q, rows_im, KA : 2 * KA] = kr
+    spread_line(1, core)
     copies = {2: finish(2, weight_items)}
-    multiply(0, slice(0, MROWS), 2 * KA)
+    arrive(1, 3, 6, 8, 10, 12, 14, 15, 16, 17, 18)
+    spread_line(1, 1 - core)
+    multiply(0, a, b, slice(0, MROWS))
     real_items = send_margins(0)
-    multiply(1, slice(MROWS, 2 * MROWS), 2 * KA)
+    multiply(1, a, b, slice(MROWS, 2 * MROWS))
     imag_items = send_margins(1)
+    for item in sent.values():
+        item.wait_send()
 
     @pl.loop(0, GRID // 128)
     def _(tile):
@@ -709,14 +726,13 @@
         @pl.loop(0, GRID // 256)
         def _(tile):
             cols = pl.ds(pl.multiple_of(tile * 256, 256), 256)
-            out_ref[c, :, cols] = jnp.dot(
-                half[c], perm[:, cols], preferred_element_type=jnp.float32
-            )
+            own = jnp.dot(half[c], perm[:, cols], preferred_element_type=jnp.float32)
+            own_ref[c, :, cols] = own.astype(jnp.bfloat16)
 
     i = lax.broadcasted_iota(jnp.int32, (256, 256), 0)
     j = lax.broadcasted_iota(jnp.int32, (256, 256), 1)
     flip = (i + j == 255).astype(jnp.float32).astype(jnp.bfloat16)
-    for c, sign in ((2, 1.0), (0, 1.0), (1, -1.0)):
+    for c in (2, 0, 1):
         copies[c].wait()
         turned = jnp.dot(flip, mirror[c], preferred_element_type=jnp.float32)
         mirror[c] = turned.astype(jnp.bfloat16)
@@ -724,62 +740,73 @@
         @pl.loop(0, GRID // 256)
         def _(tile):
             cols = pl.ds(pl.multiple_of(tile * 256, 256), 256)
-            out_ref[c, :, cols] += sign * jnp.dot(
-                mirror[c], back[:, cols], preferred_element_type=jnp.float32
-            )
-
-
-def fused(table, trig, cap, spare):
+            other = jnp.dot(mirror[c], back[:, cols], preferred_element_type=jnp.float32)
+            back_ref[c, :, cols] = other.astype(jnp.bfloat16)
+
+
+def whole(rows, table, trig, slice_re, slice_im, slice_ctf):
     vmem = pl.BlockSpec(memory_space=pltpu.VMEM)
+    dma = pltpu.SemaphoreType.DMA
+    bf16 = jnp.bfloat16
     slab = (3, ZD, LINES, GRID)
     flat = (3, ZD * LINES, GRID)
+    slots = (3, STRIP, SLICE)
     return pl.pallas_call(
-        fused_kernel,
-        out_shape=jax.ShapeDtypeStruct(flat, jnp.float32),
-        in_specs=[vmem] * 4,
-        out_specs=vmem,
+        whole_kernel,
+        out_shape=(
+            jax.ShapeDtypeStruct(flat, bf16),
+            jax.ShapeDtypeStruct(flat, bf16),
+            jax.ShapeDtypeStruct((SLABS, 8, 128), jnp.float32),
+        ),
+        in_specs=[pl.BlockSpec(memory_space=pltpu.SMEM)] + [vmem] * 5,
+        out_specs=(vmem,) * 3,
         scratch_shapes=[
-            pltpu.VMEM((2, 2 * KA, GRID), jnp.bfloat16),
-            pltpu.VMEM((2, 2 * MROWS, 2 * KA), jnp.bfloat16),
+            pltpu.VMEM((SLABS,) + slots, bf16),
+            pltpu.VMEM((SLABS,) + slots, bf16),
+            pltpu.VMEM((SLABS * SPARE,) + slots, bf16),
+            pltpu.VMEM((2, 2 * KA, GRID), bf16),
+            pltpu.VMEM((2, KA, GRID), bf16),
+            pltpu.VMEM((2, 2 * MROWS, 2 * KA), bf16),
+            pltpu.VMEM((2, MROWS, KA), bf16),
             pltpu.VMEM(slab, jnp.float32),
-            pltpu.VMEM(slab, jnp.bfloat16),
-            pltpu.VMEM(slab, jnp.bfloat16),
+            pltpu.VMEM(slab, bf16),
+            pltpu.VMEM(slab, bf16),
             pltpu.VMEM((3, 6, 8, GRID), jnp.float32),
-            pltpu.VMEM(slab, jnp.bfloat16),
-            pltpu.VMEM(slab, jnp.bfloat16),
+            pltpu.VMEM(slab, bf16),
+            pltpu.VMEM(slab, bf16),
             pltpu.VMEM((3, 6, 8, GRID), jnp.float32),
-            pltpu.VMEM(flat, jnp.bfloat16),
-            pltpu.VMEM(flat, jnp.bfloat16),
-            pltpu.VMEM((GRID, GRID), jnp.bfloat16),
-            pltpu.VMEM((GRID, GRID), jnp.bfloat16),
-            pltpu.SemaphoreType.DMA((27,)),
-            pltpu.SemaphoreType.DMA((27,)),
+            pltpu.VMEM(flat, bf16),
+            pltpu.VMEM(flat, bf16),
+            pltpu.VMEM((GRID, GRID), bf16),
+            pltpu.VMEM((GRID, GRID), bf16),
+            dma((27,)), dma((27,)), dma((2, 19)), dma((2, 19)),
+            dma((2, SLABS)), dma((2, SLABS)), dma((SLABS,)), dma((SLABS,)),
         ],
         compiler_params=pltpu.CompilerParams(
-            collective_id=3, has_side_effects=True, vmem_limit_bytes=62 << 20
+            collective_id=3, has_side_effects=True, vmem_limit_bytes=63 << 20
         ),
-        name="fused",
-    )(table, trig, cap, spare)
-
-
-def balanced(slice_re, slice_im, slice_ctf, dest, plane, helix, tilt, shift):
+        name="whole",
+    )(rows, table, trig, slice_re, slice_im, slice_ctf)
+
+
+def per_device(*arguments):
+    slice_re, slice_im, slice_ctf, dest, plane, helix, tilt, shift = arguments
     table, rows = plan(dest, plane, helix, tilt, shift)
-    cap, spare, tables = dispatch_all(rows, table, slice_re, slice_im, slice_ctf)
     band = lax.axis_index("kz") * ZD + jnp.arange(16) - MZ
     angle = twist_step * (jnp.arange(8)[None, :] * band[:, None]).astype(jnp.float32)
     trig = jnp.concatenate([jnp.cos(angle), jnp.sin(angle)], axis=1)
-    fits = jnp.max(tables[:, 0, EXTRA]) <= SPARE
-    return tables.reshape(SLABS * 8, 128), trig, cap, spare, fits
-
-
-def per_device(*arguments):
-    table, trig, cap, spare, fits = balanced(*arguments)
-    out = lax.cond(
-        fits,
-        lambda: fused(table, trig, cap, spare),
-        lambda: padded(*arguments),
+    own, back, tables = whole(rows, table, trig, slice_re, slice_im, slice_ctf)
+    signs = jnp.array([1.0, -1.0, 1.0], jnp.float32).reshape(3, 1, 1)
+
+    def fold(own, back):
+        out = own.astype(jnp.float32) + signs * back.astype(jnp.float32)
+        return out.reshape(3, ZD, LINES, GRID)
+
+    return lax.cond(
+        jnp.max(tables[:, 0, EXTRA]) <= SPARE,
+        lambda: fold(own, back),
+        lambda: fold(*padded(*arguments)),
     )
-    return out.reshape(3, ZD, LINES, GRID)
 
 
 def solution(mesh):

time: 182 us -> 169 us (0.929); the launches traced: 182 us -> 167 us
  Pallas kernels: 171 us -> 156 us
  local copies, waits for them, and re-layouts: 6.81 us -> 1.66 us
  other arithmetic: 3.25 us -> 7.66 us
    pallas_call x2 -> x1, Pallas kernels: 169 us -> 154 us  [whole(): pl.pallas_call(whole_kernel, out_shape=(jax.ShapeDtypeStruct(flat, bf16),...]
    unnamed x6 -> x2, local copies, waits for them, and re-layouts: 6.81 us -> 1.66 us
    add x0 -> x1, other arithmetic: none -> 2.77 us  [fold(): out = own.astype(jnp.float32) + signs * back.astype(jnp.float32)]
where the time goes in v3:
time: 169 us; the launch traced here: 167 us
  Pallas kernels  156 us (92%)
  other arithmetic  7.66 us (5%)
    pallas_call x1, Pallas kernels, whole(): pl.pallas_call(whole_kernel, out_shape=(jax.ShapeDtypeStruct(flat, bf16),...  154 us

profile of v3, /device:TPU:1, one launch (start us, length us, event | category | flops | bytes accessed | tf_op | source)
XLA Modules:
  0.0 166.5 jit_solution(16403315254034107893)
XLA Ops:
  0.0 0.1 fusion.11
  0.1 0.7 pad_maximum_fusion.2.trig
  0.8 1.3 maximum_convert_fusion.reals
  2.1 1.3 pad_add_fusion.numbers
  3.4 1.9 %plan.1 = (f32[16,8,128]{2,1,0:T(8,128)}, s32[32]{0:T(128)}) custom-call(s32[3,16]{1,0:T(4,128)} %pad_add_fusion.numbers, f32[3,16]{1,0:T(4,128)} %maximum_convert_fusion.reals), custom_call_target="tpu_custom_call" | custom-call | tf_op jit(solution)/shard_map/plan/pallas_call | solution.py:386
  5.3 154.4 %whole.1 = (bf16[3,256,1024]{2,1,0:T(8,128)(2,1)}, bf16[3,256,1024]{2,1,0:T(8,128)(2,1)}, f32[16,8,128]{2,1,0:T(8,128)}) custom-call(s32[32]{0:T(128)} %get-tuple-element.64.rows, f32[16,8,128]{2,1,0:T(8,128)} %get-tuple-element.65.table, f32[16,16]{1,0:T(8,128)} %pad_maximum_fusion.2.trig, bf16[16,32,512]{2,1,0:T(8,128)(2,1)} %re_ref.1, ...), custom_call_target="tpu_custom_call" | custom-call | tf_op jit(solution)/shard_map/whole/pallas_call | solution.py:754
  159.6 1.5 slice_reduce_fusion.1
  161.8 3.0 %conditional.1 = (f32[3,4,64,1024]{3,2,1,0:T(8,128)S(1)}) conditional(s32[]{:T(128)} %convert_element_type.101, ((), s32[16,1]{0,1:T(1,128)}, s32[16]{0:T(128)}, s32[16]{0:T(128)}, bf16[16]{0:T(256)(128)(2,1)}, /*index=5*/bf16[2,16]{1,0:T(2,128)(2,1)}, bf16[16,32,512]{2,1,0:T(8,128)(2,1)}, bf16[16,32,512]{2,1,0:T(8,128)(2,1)}, ...), branch_computations={%region_1.6_spmd, %region_6.7_spmd} | conditional | flops 11953012736 | bytes 132726472 | solution.py:805
  162.1 2.8 %multiply_add_fusion = f32[3,256,1024]{2,1,0:T(8,128)S(1)} fusion(bf16[3,256,1024]{2,1,0:T(8,128)(2,1)} %get-tuple-element.58, bf16[3,256,1024]{2,1,0:T(8,128)(2,1)} %get-tuple-element.56, f32[3]{0:T(128)} %bitcast.46), kind=kLoop, calls=%fused_computation.3 | loop fusion | flops 3145728 | bytes 6291468 | tf_op jit(solution)/shard_map/cond/branch_1_fun/add | solution.py:802
  164.8 0.0 copy-start
  164.8 1.7 copy-done
  (1 shorter events, 0.0 us)
Async XLA Ops:
  164.8 1.7 %copy-start = (f32[3,4,64,1024]{3,2,1,0:T(8,128)}, f32[3,4,64,1024]{3,2,1,0:T(8,128)S(1)}, u32[]{:S(2)}) copy-start(f32[3,4,64,1024]{3,2,1,0:T(8,128)S(1)} %get-tuple-element.89) | copy-start | bytes 9437188

commit v4 on v3

--- a/solution.py
+++ b/solution.py
@@ -337,71 +337,9 @@
 PLANE, HELIX, VALID, TILT, SHIFT_Y, SHIFT_X, DEST, TAPS, EXTRA = 0, 1, 2, 3, 4, 5, 6, 8, 12
 
 
-def plan_kernel(numbers, reals, table, rows, seen):
-    lane = lax.broadcasted_iota(jnp.int32, (1, 128), 1)
-    table[...] = jnp.zeros_like(table)
-    for d in range(SLABS):
-        seen[d] = 0
-        rows[d] = 0
-        rows[SLABS + d] = 0
-    extra = jnp.int32(0)
-    for i in range(SLABS):
-        d = numbers[0, i]
-        fields = (
-            (PLANE, numbers[1, i].astype(jnp.float32)),
-            (HELIX, numbers[2, i].astype(jnp.float32)),
-            (VALID, 1.0), (TILT, reals[0, i]), (SHIFT_Y, reals[1, i]), (SHIFT_X, reals[2, i]),
-            (DEST, d.astype(jnp.float32)),
-        )
-        row = jnp.zeros((1, 128), jnp.float32)
-        for index, value in fields:
-            row = jnp.where(lane == index, value, row)
-        before = seen[d]
-
-        @pl.when(before == 0)
-        def _():
-            table[d, 0:1, :] = row
-            rows[d] = i
-
-        @pl.when((before > 0) & (extra < SPARE))
-        def _():
-            rows[SLABS + extra] = i
-            for other in range(SLABS):
-                table[other, pl.ds(1 + extra, 1), :] = row
-
-        seen[d] = before + 1
-        extra = extra + jnp.where(before > 0, 1, 0)
-    lags = jnp.where(lane == TAPS + 1, 2.0, jnp.where(lane == TAPS + 2, 1.0, 0.0))
-    lags = jnp.where(lane == TAPS + 3, -1.0, lags)
-    for d in range(SLABS):
-        block = table[d]
-        taps = kaiser(lags - block[:, SHIFT_X : SHIFT_X + 1])
-        taps = taps.astype(jnp.bfloat16).astype(jnp.float32)
-        block = jnp.where((lane >= TAPS) & (lane < TAPS + 4), taps, block)
-        table[d] = jnp.where(lane == EXTRA, extra.astype(jnp.float32), block)
-
-
-def plan(dest, plane, helix, tilt, shift):
-    smem = pl.BlockSpec(memory_space=pltpu.SMEM)
-    return pl.pallas_call(
-        plan_kernel,
-        out_shape=(
-            jax.ShapeDtypeStruct((SLABS, 8, 128), jnp.float32),
-            jax.ShapeDtypeStruct((2 * SLABS,), jnp.int32),
-        ),
-        in_specs=[smem] * 2,
-        out_specs=(pl.BlockSpec(memory_space=pltpu.VMEM), smem),
-        scratch_shapes=[pltpu.SMEM((SLABS,), jnp.int32)],
-        name="plan",
-    )(
-        jnp.stack([dest[:, 0], plane, helix]),
-        jnp.concatenate([tilt[None], shift], axis=0).astype(jnp.float32),
-    )
-
-
 def whole_kernel(
-    rows, table, trig, re_ref, im_ref, ctf_ref, own_ref, back_ref, tables,
-    outbox, cap, spare, b, bw, a, aw, mid, up, dn, edge, from_low, from_high, halos, half, mirror,
+    dest, dest_line, plane_line, helix_line, tilt_line, shift_lines, re_ref, im_ref, ctf_ref,
+    own_ref, back_ref, flag_ref, tables, table, held, rows, outbox, cap, spare, b, bw, a, aw, mid, up, dn, edge, from_low, from_high, halos, half, mirror,
     perm, back, send, recv, hop_send, hop_recv, cap_send, cap_recv, tab_send, tab_recv,
 ):
     kz, ky = lax.axis_index("kz"), lax.axis_index("ky")
@@ -428,6 +366,22 @@
     for peer in peers:
         pl.semaphore_signal(barrier, inc=1, device_id=peer, device_id_type=MESH)
 
+    first = []
+    for d in range(SLABS):
+        found = jnp.int32(SLABS)
+        for i in reversed(range(SLABS)):
+            found = jnp.where(dest[i] == d, i, found)
+        first.append(found)
+    extra = jnp.int32(0)
+    spare_rows = [jnp.int32(0)] * SPARE
+    for i in range(1, SLABS):
+        again = dest[i] == dest[0]
+        for earlier in range(1, i):
+            again = again | (dest[i] == dest[earlier])
+        for j in range(SPARE):
+            spare_rows[j] = jnp.where(again & (extra == j), i, spare_rows[j])
+        extra = extra + jnp.where(again, 1, 0)
+
     def pack_signal(row, target, place):
         ctf = ctf_ref[row].astype(jnp.float32)
         target[place, 0] = (ctf * re_ref[row].astype(jnp.float32)).astype(jnp.bfloat16)
@@ -438,7 +392,43 @@
         target[place, 2] = (ctf * ctf).astype(jnp.bfloat16)
 
     for j in range(SPARE):
-        pack_weight(rows[SLABS + j], spare, kz * SPARE + j)
+        pack_weight(spare_rows[j], spare, kz * SPARE + j)
+
+    lane = lax.broadcasted_iota(jnp.int32, (1, 128), 1)
+    kind = lax.broadcasted_iota(jnp.int32, (8, SLABS), 0)
+    fields = jnp.where(kind == VALID, 1.0, 0.0)
+    shifts = shift_lines[...].astype(jnp.float32)
+    for index, value in (
+        (PLANE, plane_line[...].astype(jnp.float32)),
+        (HELIX, helix_line[...].astype(jnp.float32)),
+        (TILT, tilt_line[...].astype(jnp.float32)), (SHIFT_Y, shifts[0:1]),
+        (SHIFT_X, shifts[1:2]), (DEST, dest_line[...].astype(jnp.float32)),
+    ):
+        fields = jnp.where(kind == index, value, fields)
+    same = lax.broadcasted_iota(jnp.int32, (8, 128), 0) == lax.broadcasted_iota(
+        jnp.int32, (8, 128), 1
+    )
+    notes = lax.dot_general(
+        fields.astype(jnp.bfloat16), same.astype(jnp.float32).astype(jnp.bfloat16),
+        (((0,), (0,)), ((), ())), preferred_element_type=jnp.float32,
+    )
+    lags = jnp.where(lane == TAPS + 1, 2.0, jnp.where(lane == TAPS + 2, 1.0, 0.0))
+    lags = jnp.where(lane == TAPS + 3, -1.0, lags)
+    taps = kaiser(lags - notes[:, SHIFT_X : SHIFT_X + 1])
+    taps = taps.astype(jnp.bfloat16).astype(jnp.float32)
+    held[...] = jnp.where((lane >= TAPS) & (lane < TAPS + 4), taps, notes)
+    count = extra.astype(jnp.float32)
+    shared = [jnp.zeros((1, 128), jnp.float32)]
+    for j in range(SPARE):
+        shared.append(jnp.where(extra > j, 1.0, 0.0) * held[pl.ds(spare_rows[j], 1), :])
+    for d in range(SLABS):
+        there = jnp.where(first[d] < SLABS, 1.0, 0.0)
+        first[d] = jnp.where(first[d] < SLABS, first[d], 0)
+        shared[0] = there * held[pl.ds(first[d], 1), :]
+        for j in range(1 + SPARE):
+            table[d, j : j + 1, :] = jnp.where(lane == EXTRA, count, shared[j])
+        table[d, 1 + SPARE : 8, :] = jnp.zeros((7 - SPARE, 128), jnp.float32)
+        rows[d] = first[d]
     pl.semaphore_wait(barrier, len(peers))
 
     channels = (slice(2, 3), slice(0, 2))
@@ -521,15 +511,15 @@
         item.start()
         labels.append(item)
     tables[kz] = table[kz]
+    for j in range(SPARE):
+        pack_signal(spare_rows[j], spare, kz * SPARE + j)
+    hop_two(0)
     send_caps(0, pack_weight)
-    for j in range(SPARE):
-        pack_signal(rows[SLABS + j], spare, kz * SPARE + j)
-    hop_two(0)
     hop_one(1)
-    send_caps(1, pack_signal)
     hop_three(0)
     for item in labels:
         item.wait()
+    flag_ref[...] = jnp.max(tables[...], axis=0)
 
     k = lax.broadcasted_iota(jnp.int32, (1, KA), 1)
     slot, local = k // HALF, k % HALF
@@ -551,11 +541,15 @@
     main_y = kaiser((line - 2 * local).astype(jnp.float32) - shift)
     low_y = kaiser((-1 - 2 * local).astype(jnp.float32) - shift)
     high_y = kaiser((32 - 2 * local).astype(jnp.float32) - shift)
+    helices = lax.broadcasted_iota(jnp.int32, (16, 128), 1)
+    bands = lax.broadcasted_iota(jnp.int32, (16, 128), 0) + kz * ZD - MZ
+    angle = twist_step * (helices * bands).astype(jnp.float32)
+    cos_of, sin_of = jnp.cos(angle), jnp.sin(angle)
     cosine = jnp.zeros((16, KA), jnp.float32)
     sine = jnp.zeros((16, KA), jnp.float32)
     for h in range(8):
-        cosine = jnp.where(helix == float(h), trig[:, h : h + 1], cosine)
-        sine = jnp.where(helix == float(h), trig[:, 8 + h : 9 + h], sine)
+        cosine = jnp.where(helix == float(h), cos_of[:, h : h + 1], cosine)
+        sine = jnp.where(helix == float(h), sin_of[:, h : h + 1], sine)
 
     def along_z(q):
         row = ky * STRIP + q * HALF + local - SLICE // 2
@@ -676,6 +670,7 @@
             aw[q, first : first + size, :] = (along[levels] * value_y).astype(jnp.bfloat16)
     hop_four(0)
     hop_two(1)
+    send_caps(1, pack_signal)
     spread_caps(0)
     spread_line(0, core)
     arrive(0, 3, 6, 8, 10, 12, 14, 15, 16, 17, 18)
@@ -744,7 +739,7 @@
             back_ref[c, :, cols] = other.astype(jnp.bfloat16)
 
 
-def whole(rows, table, trig, slice_re, slice_im, slice_ctf):
+def whole(dest, plane, helix, tilt, shift, slice_re, slice_im, slice_ctf):
     vmem = pl.BlockSpec(memory_space=pltpu.VMEM)
     dma = pltpu.SemaphoreType.DMA
     bf16 = jnp.bfloat16
@@ -756,11 +751,15 @@
         out_shape=(
             jax.ShapeDtypeStruct(flat, bf16),
             jax.ShapeDtypeStruct(flat, bf16),
-            jax.ShapeDtypeStruct((SLABS, 8, 128), jnp.float32),
+            jax.ShapeDtypeStruct((8, 128), jnp.float32),
         ),
-        in_specs=[pl.BlockSpec(memory_space=pltpu.SMEM)] + [vmem] * 5,
+        in_specs=[pl.BlockSpec(memory_space=pltpu.SMEM)] + [vmem] * 8,
         out_specs=(vmem,) * 3,
         scratch_shapes=[
+            pltpu.VMEM((SLABS, 8, 128), jnp.float32),
+            pltpu.VMEM((SLABS, 8, 128), jnp.float32),
+            pltpu.VMEM((SLABS, 128), jnp.float32),
+            pltpu.SMEM((SLABS,), jnp.int32),
             pltpu.VMEM((SLABS,) + slots, bf16),
             pltpu.VMEM((SLABS,) + slots, bf16),
             pltpu.VMEM((SLABS * SPARE,) + slots, bf16),
@@ -786,16 +785,15 @@
             collective_id=3, has_side_effects=True, vmem_limit_bytes=63 << 20
         ),
         name="whole",
-    )(rows, table, trig, slice_re, slice_im, slice_ctf)
+    )(
+        dest.reshape(SLABS), dest.reshape(1, SLABS), plane.reshape(1, SLABS),
+        helix.reshape(1, SLABS), tilt.reshape(1, SLABS), shift, slice_re, slice_im, slice_ctf,
+    )
 
 
 def per_device(*arguments):
     slice_re, slice_im, slice_ctf, dest, plane, helix, tilt, shift = arguments
-    table, rows = plan(dest, plane, helix, tilt, shift)
-    band = lax.axis_index("kz") * ZD + jnp.arange(16) - MZ
-    angle = twist_step * (jnp.arange(8)[None, :] * band[:, None]).astype(jnp.float32)
-    trig = jnp.concatenate([jnp.cos(angle), jnp.sin(angle)], axis=1)
-    own, back, tables = whole(rows, table, trig, slice_re, slice_im, slice_ctf)
+    own, back, flag = whole(dest, plane, helix, tilt, shift, slice_re, slice_im, slice_ctf)
     signs = jnp.array([1.0, -1.0, 1.0], jnp.float32).reshape(3, 1, 1)
 
     def fold(own, back):
@@ -803,7 +801,7 @@
         return out.reshape(3, ZD, LINES, GRID)
 
     return lax.cond(
-        jnp.max(tables[:, 0, EXTRA]) <= SPARE,
+        flag[0, EXTRA] <= SPARE,
         lambda: fold(own, back),
         lambda: fold(*padded(*arguments)),
     )

time: 169 us -> 163 us (0.964)
  the two profiles are of different devices: /device:TPU:1 before, /device:TPU:16 now
where the time goes in v4:
time: 163 us
  Pallas kernels  156 us (96%)
  local copies, waits for them, and re-layouts  2.92 us (2%)
  other arithmetic  2.77 us (2%)
    pallas_call x1, Pallas kernels, whole(): pl.pallas_call(whole_kernel, out_shape=(jax.ShapeDtypeStruct(flat, bf16),...  156 us

profile of v4, /device:TPU:16, one launch (start us, length us, event | category | flops | bytes accessed | tf_op | source)
XLA Modules:
  0.0 162.9 jit_solution(6411528967105349808)
XLA Ops:
  0.0 156.3 %whole.1 = (bf16[3,256,1024]{2,1,0:T(8,128)(2,1)}, bf16[3,256,1024]{2,1,0:T(8,128)(2,1)}, f32[8,128]{1,0:T(8,128)}) custom-call(s32[16]{0:T(128)} %bitcast.44, s32[1,16]{1,0:T(1,128)} %bitcast.45, s32[1,16]{1,0:T(1,128)} %bitcast.52, s32[1,16]{1,0:T(1,128)} %bitcast.53, bf16[1,16]{1,0:T(2,128)(2,1)} %bitcast.50, bf16[2,16]{1,0:T(2,128)(2,1)} %shift_lines.1, ...), custom_call_target="tpu_custom_call" | custom-call | tf_op jit(solution)/shard_map/whole/pallas_call | solution.py:749
  156.3 1.3 slice.15
  158.2 3.0 %conditional.1 = (f32[3,4,64,1024]{3,2,1,0:T(8,128)S(1)}) conditional(s32[]{:T(128)} %bitcast.26, ((), s32[16,1]{0,1:T(1,128)}, s32[16]{0:T(128)}, s32[16]{0:T(128)}, bf16[16]{0:T(256)(128)(2,1)}, /*index=5*/bf16[2,16]{1,0:T(2,128)(2,1)}, bf16[16,32,512]{2,1,0:T(8,128)(2,1)}, bf16[16,32,512]{2,1,0:T(8,128)(2,1)}, bf16[16,32,512]{2,1,0:T(8,128)(2,1)}, ...), branch_computations={%region_0.5_spmd, %region_5.6_spmd} | conditional | flops 11953012736 | bytes 132726472 | solution.py:803
  158.4 2.8 %multiply_add_fusion = f32[3,256,1024]{2,1,0:T(8,128)S(1)} fusion(bf16[3,256,1024]{2,1,0:T(8,128)(2,1)} %get-tuple-element.58, bf16[3,256,1024]{2,1,0:T(8,128)(2,1)} %get-tuple-element.56, f32[3]{0:T(128)} %bitcast.49), kind=kLoop, calls=%fused_computation.3 | loop fusion | flops 3145728 | bytes 6291468 | tf_op jit(solution)/shard_map/cond/branch_1_fun/add | solution.py:800
  161.2 0.0 copy-start
  161.2 1.7 %copy-done = f32[3,4,64,1024]{3,2,1,0:T(8,128)} copy-done((f32[3,4,64,1024]{3,2,1,0:T(8,128)}, f32[3,4,64,1024]{3,2,1,0:T(8,128)S(1)}, u32[]{:S(2)}) %copy-start) | copy-done | bytes 3145752
Async XLA Ops:
  161.2 1.7 %copy-start = (f32[3,4,64,1024]{3,2,1,0:T(8,128)}, f32[3,4,64,1024]{3,2,1,0:T(8,128)S(1)}, u32[]{:S(2)}) copy-start(f32[3,4,64,1024]{3,2,1,0:T(8,128)S(1)} %get-tuple-element.83) | copy-start | bytes 9437188

commit v5 on v4

--- a/solution.py
+++ b/solution.py
@@ -679,6 +679,7 @@
     multiply(2, aw, bw, slice(0, MROWS))
     weight_items = send_margins(2)
     hop_four(1)
+    copies = {2: finish(2, weight_items)}
     spread_caps(1)
     for q in range(2):
         along = along_z(q)
@@ -694,7 +695,6 @@
             a[q, rows_im, 0:KA] = ki.astype(jnp.bfloat16)
             a[q, rows_im, KA : 2 * KA] = kr
     spread_line(1, core)
-    copies = {2: finish(2, weight_items)}
     arrive(1, 3, 6, 8, 10, 12, 14, 15, 16, 17, 18)
     spread_line(1, 1 - core)
     multiply(0, a, b, slice(0, MROWS))

time: 163 us -> 157 us (0.963)
  the two profiles are of different devices: /device:TPU:16 before, /device:TPU:1 now
where the time goes in v5:
time: 157 us; the launch traced here: 156 us
  Pallas kernels  150 us (96%)
  local copies, waits for them, and re-layouts  2.92 us (2%)
  other arithmetic  2.77 us (2%)
    pallas_call x1, Pallas kernels, whole(): pl.pallas_call(whole_kernel, out_shape=(jax.ShapeDtypeStruct(flat, bf16),...  150 us

profile of v5, /device:TPU:1, one launch (start us, length us, event | category | flops | bytes accessed | tf_op | source)
XLA Modules:
  0.0 156.2 jit_solution(12096758162372910788)
XLA Ops:
  0.0 149.5 %whole.1 = (bf16[3,256,1024]{2,1,0:T(8,128)(2,1)}, bf16[3,256,1024]{2,1,0:T(8,128)(2,1)}, f32[8,128]{1,0:T(8,128)}) custom-call(s32[16]{0:T(128)} %bitcast.44, s32[1,16]{1,0:T(1,128)} %bitcast.45, s32[1,16]{1,0:T(1,128)} %bitcast.52, s32[1,16]{1,0:T(1,128)} %bitcast.53, bf16[1,16]{1,0:T(2,128)(2,1)} %bitcast.50, bf16[2,16]{1,0:T(2,128)(2,1)} %shift_lines.1, ...), custom_call_target="tpu_custom_call" | custom-call | tf_op jit(solution)/shard_map/whole/pallas_call | solution.py:749
  149.5 1.3 slice.15
  151.5 3.0 %conditional.1 = (f32[3,4,64,1024]{3,2,1,0:T(8,128)S(1)}) conditional(s32[]{:T(128)} %bitcast.26, ((), s32[16,1]{0,1:T(1,128)}, s32[16]{0:T(128)}, s32[16]{0:T(128)}, bf16[16]{0:T(256)(128)(2,1)}, /*index=5*/bf16[2,16]{1,0:T(2,128)(2,1)}, bf16[16,32,512]{2,1,0:T(8,128)(2,1)}, bf16[16,32,512]{2,1,0:T(8,128)(2,1)}, bf16[16,32,512]{2,1,0:T(8,128)(2,1)}, ...), branch_computations={%region_0.5_spmd, %region_5.6_spmd} | conditional | flops 11953012736 | bytes 132726472 | solution.py:803
  151.7 2.8 %multiply_add_fusion = f32[3,256,1024]{2,1,0:T(8,128)S(1)} fusion(bf16[3,256,1024]{2,1,0:T(8,128)(2,1)} %get-tuple-element.58, bf16[3,256,1024]{2,1,0:T(8,128)(2,1)} %get-tuple-element.56, f32[3]{0:T(128)} %bitcast.49), kind=kLoop, calls=%fused_computation.3 | loop fusion | flops 3145728 | bytes 6291468 | tf_op jit(solution)/shard_map/cond/branch_1_fun/add | solution.py:800
  154.5 0.0 copy-start
  154.5 1.7 %copy-done = f32[3,4,64,1024]{3,2,1,0:T(8,128)} copy-done((f32[3,4,64,1024]{3,2,1,0:T(8,128)}, f32[3,4,64,1024]{3,2,1,0:T(8,128)S(1)}, u32[]{:S(2)}) %copy-start) | copy-done | bytes 3145752
Async XLA Ops:
  154.5 1.7 %copy-start = (f32[3,4,64,1024]{3,2,1,0:T(8,128)}, f32[3,4,64,1024]{3,2,1,0:T(8,128)S(1)}, u32[]{:S(2)}) copy-start(f32[3,4,64,1024]{3,2,1,0:T(8,128)S(1)} %get-tuple-element.83) | copy-start | bytes 9437188

commit v6 on v5

--- a/solution.py
+++ b/solution.py
@@ -695,6 +695,16 @@
             a[q, rows_im, 0:KA] = ki.astype(jnp.bfloat16)
             a[q, rows_im, KA : 2 * KA] = kr
     spread_line(1, core)
+
+    @pl.loop(0, GRID // 128)
+    def _(tile):
+        rows = pl.multiple_of(tile * 128, 128)
+        k = lax.broadcasted_iota(jnp.int32, (128, GRID), 0) + rows
+        x = lax.broadcasted_iota(jnp.int32, (128, GRID), 1)
+        wanted = jnp.where(k < SLICE, 2 * k, 2 * (k - SLICE) + 1)
+        perm[pl.ds(rows, 128), :] = (x == wanted).astype(jnp.float32).astype(jnp.bfloat16)
+        back[pl.ds(rows, 128), :] = (GRID - 1 - x == wanted).astype(jnp.float32).astype(jnp.bfloat16)
+
     arrive(1, 3, 6, 8, 10, 12, 14, 15, 16, 17, 18)
     spread_line(1, 1 - core)
     multiply(0, a, b, slice(0, MROWS))
@@ -703,15 +713,6 @@
     imag_items = send_margins(1)
     for item in sent.values():
         item.wait_send()
-
-    @pl.loop(0, GRID // 128)
-    def _(tile):
-        rows = pl.multiple_of(tile * 128, 128)
-        k = lax.broadcasted_iota(jnp.int32, (128, GRID), 0) + rows
-        x = lax.broadcasted_iota(jnp.int32, (128, GRID), 1)
-        wanted = jnp.where(k < SLICE, 2 * k, 2 * (k - SLICE) + 1)
-        perm[pl.ds(rows, 128), :] = (x == wanted).astype(jnp.float32).astype(jnp.bfloat16)
-        back[pl.ds(rows, 128), :] = (GRID - 1 - x == wanted).astype(jnp.float32).astype(jnp.bfloat16)
 
     copies[0] = finish(0, real_items)
     copies[1] = finish(1, imag_items)

time: 157 us -> 159 us (1.013)
  the two profiles are of different devices: /device:TPU:1 before, /device:TPU:7 now
where the time goes in v6:
time: 159 us
  Pallas kernels  152 us (96%)
  local copies, waits for them, and re-layouts  2.92 us (2%)
  other arithmetic  2.77 us (2%)
    pallas_call x1, Pallas kernels, whole(): pl.pallas_call(whole_kernel, out_shape=(jax.ShapeDtypeStruct(flat, bf16),...  152 us

profile of v6, /device:TPU:7, one launch (start us, length us, event | category | flops | bytes accessed | tf_op | source)
XLA Modules:
  0.0 158.7 jit_solution(15584917925543387235)
XLA Ops:
  0.0 152.1 %whole.1 = (bf16[3,256,1024]{2,1,0:T(8,128)(2,1)}, bf16[3,256,1024]{2,1,0:T(8,128)(2,1)}, f32[8,128]{1,0:T(8,128)}) custom-call(s32[16]{0:T(128)} %bitcast.44, s32[1,16]{1,0:T(1,128)} %bitcast.45, s32[1,16]{1,0:T(1,128)} %bitcast.52, s32[1,16]{1,0:T(1,128)} %bitcast.53, bf16[1,16]{1,0:T(2,128)(2,1)} %bitcast.50, bf16[2,16]{1,0:T(2,128)(2,1)} %shift_lines.1, ...), custom_call_target="tpu_custom_call" | custom-call | tf_op jit(solution)/shard_map/whole/pallas_call | solution.py:750
  152.1 1.3 slice.15
  154.0 3.0 %conditional.1 = (f32[3,4,64,1024]{3,2,1,0:T(8,128)S(1)}) conditional(s32[]{:T(128)} %bitcast.26, ((), s32[16,1]{0,1:T(1,128)}, s32[16]{0:T(128)}, s32[16]{0:T(128)}, bf16[16]{0:T(256)(128)(2,1)}, /*index=5*/bf16[2,16]{1,0:T(2,128)(2,1)}, bf16[16,32,512]{2,1,0:T(8,128)(2,1)}, bf16[16,32,512]{2,1,0:T(8,128)(2,1)}, bf16[16,32,512]{2,1,0:T(8,128)(2,1)}, ...), branch_computations={%region_0.5_spmd, %region_5.6_spmd} | conditional | flops 11953012736 | bytes 132726472 | solution.py:804
  154.3 2.8 %multiply_add_fusion = f32[3,256,1024]{2,1,0:T(8,128)S(1)} fusion(bf16[3,256,1024]{2,1,0:T(8,128)(2,1)} %get-tuple-element.58, bf16[3,256,1024]{2,1,0:T(8,128)(2,1)} %get-tuple-element.56, f32[3]{0:T(128)} %bitcast.49), kind=kLoop, calls=%fused_computation.3 | loop fusion | flops 3145728 | bytes 6291468 | tf_op jit(solution)/shard_map/cond/branch_1_fun/add | solution.py:801
  157.0 0.0 copy-start
  157.1 1.7 %copy-done = f32[3,4,64,1024]{3,2,1,0:T(8,128)} copy-done((f32[3,4,64,1024]{3,2,1,0:T(8,128)}, f32[3,4,64,1024]{3,2,1,0:T(8,128)S(1)}, u32[]{:S(2)}) %copy-start) | copy-done | bytes 3145752
Async XLA Ops:
  157.0 1.7 %copy-start = (f32[3,4,64,1024]{3,2,1,0:T(8,128)}, f32[3,4,64,1024]{3,2,1,0:T(8,128)S(1)}, u32[]{:S(2)}) copy-start(f32[3,4,64,1024]{3,2,1,0:T(8,128)S(1)} %get-tuple-element.83) | copy-start | bytes 9437188
